TPU v7x, 32 devices: a whole 2x2x4 slice. The times are simulated.
32 devices in a mesh: sep: 4 (over y, x), gx: 8 (over z, core).
Axes of the slice: x: 2, y: 2, z: 4, core: 2. Of those that a mesh axis runs over, the one named last changes fastest.
Arguments:
- velocity: float32 [3, 2048, 8, 128], P(None, 'gx'), may hold values from -6 to 6
- distances: int32 [32], replicated, may hold values from 1 to 2044, as said below
Outputs:
- flux_slope: float32 [32, 2048, 8, 128], P('sep', 'gx')
- transport: float32 [32, 2048, 8, 128], P('sep', 'gx')
Inputs may be any that keep to these rules, and one draw needn't show every extreme that they name: `distances`: strictly increasing. In each of the 4 groups of 8 consecutive entries, the last exceeds the first by at most (7) * 4, with equality in some group.
All inputs are finite; a program needn't handle non-finite values.
Results may differ from a plain program's by a relative error of at most 0.0003.
Values sent between devices are 32-bit elements; how exact they have to be, the bound alone decides.
No kernel may reach another device: no remote copies, remote signals or barrier semaphores. Data moves between devices by JAX's collectives and lax.ppermute only.
A program may use at most 128 MiB of HBM per device.

v0:
```python
import jax
import jax.numpy as jnp
from jax import lax
from jax.sharding import PartitionSpec as P

SEP_DEV = 8


def with_halo(block, sides, width, periodic):
    for axis, dim in sides:
        count = lax.axis_size(axis)
        forward = [(i, i + 1) for i in range(count - 1)]
        if periodic:
            forward.append((count - 1, 0))
        backward = [(target, source) for source, target in forward]
        low = lax.ppermute(
            lax.slice_in_dim(block, block.shape[dim] - width, None, axis=dim), axis, forward
        )
        high = lax.ppermute(lax.slice_in_dim(block, 0, width, axis=dim), axis, backward)
        block = jnp.concatenate([low, block, high], axis=dim)
    return block


def terms(base, moved):
    change = moved - base
    squared = jnp.sum(change * change, axis=0)
    flux = change[0] * squared
    carried = 0.5 * (moved[0] + base[0]) * squared
    return (flux, carried)


def body(velocity, distances):
    group = lax.axis_index("sep")
    groups = lax.axis_size("sep")
    cells = velocity.shape[1]
    width = lax.axis_size("gx")
    mine = lax.dynamic_slice_in_dim(distances, group * SEP_DEV, SEP_DEV)
    start = mine[0] - 1
    blocks = start // cells
    remain = start % cells
    whole = lax.all_gather(velocity, "gx", axis=1, tiled=True)
    doubled = jnp.concatenate([whole, whole[:, : 2 * cells]], axis=1)
    begin = (lax.axis_index("gx") + blocks) % width * cells
    extended = lax.dynamic_slice_in_dim(doubled, begin, 3 * cells, 1)
    flux_list = []
    slope_parts = []
    padded = with_halo(velocity, (("gx", 1),), 1, True)
    for member in range(SEP_DEV):
        offset = mine[member] - start
        moved = lax.dynamic_slice_in_dim(extended, remain + offset - 1, cells + 2, 1)
        flux, carried = terms(padded, moved)
        flux_list.append(flux[1:-1])
        slope_parts.append(0.5 * (carried[2:] - carried[:-2]))
    transport = jnp.stack(slope_parts, axis=0)
    fluxes = jnp.stack(flux_list, axis=0)
    bordered = with_halo(fluxes, (("sep", 0),), 1, False)
    below = bordered[:-2]
    above = bordered[2:]
    prefixed = jnp.concatenate([jnp.zeros((1,), jnp.int32), distances], axis=0)
    lower_dist = lax.dynamic_slice_in_dim(prefixed, group * SEP_DEV, SEP_DEV)
    appended = jnp.concatenate([distances, distances[-1:]], axis=0)
    upper_dist = lax.dynamic_slice_in_dim(appended, group * SEP_DEV + 1, SEP_DEV)
    topmost = jnp.logical_and(group == groups - 1, jnp.arange(SEP_DEV) == SEP_DEV - 1)
    above = jnp.where(topmost[:, None, None, None], fluxes, above)
    spread = (upper_dist - lower_dist).astype(jnp.float32)[:, None, None, None]
    flux_slope = (above - below) / spread
    return (flux_slope, transport)


def solution(mesh):
    placed = (P(None, "gx", None, None), P())
    return jax.shard_map(
        body,
        mesh=mesh,
        in_specs=placed,
        out_specs=(P("sep", "gx", None, None), P("sep", "gx", None, None)),
        check_vma=False,
    )
```

profile of v0, /device:TPU:4, one launch (start us, length us, event | category | flops | bytes accessed | tf_op | source)
XLA Modules:
  0.0 345.3 jit_solution(11698410467165361571)
XLA Ops:
  7.2 0.7 all-gather.2.cloned.1.call-update
  7.9 0.7 fusion.74
  8.6 3.0 collective-permute-start.1
  11.7 0.6 slice.198
  12.3 0.7 pad_add_fusion
  13.1 0.7 fusion.75
  19.1 2.6 constant_dynamic-update-slice_fusion.1
  21.7 208.9 %all-gather.2.cloned.1.call-done = f32[3,2048,8,128]{3,2,1,0:T(8,128)} async-done(((f32[3,256,8,128]{3,2,1,0:T(8,128)}), f32[3,2048,8,128]{3,2,1,0:T(8,128)}) %all-gather.2.cloned.1.call-update) | async-done | bytes 25165840 | tf_op jit(solution)/shard_map/all_gather | solution.py:41
  230.7 5.9 %slice.224 = f32[3,512,8,128]{3,2,1,0:T(8,128)} slice(f32[3,2048,8,128]{3,2,1,0:T(8,128)} %all-gather.2.cloned.1.call-done), slice={[0:3], [0:512], [0:8], [0:128]} | slice | bytes 12582912 | tf_op jit(solution)/shard_map/slice | solution.py:42
  236.6 22.7 %multiply_reduce_fusion.7 = (f32[258,8,128]{2,1,0:T(8,128)}, f32[3,258,8,128]{3,2,1,0:T(8,128)}, f32[3,258,8,128]{3,2,1,0:T(8,128)}, f32[258,8,128]{2,1,0:T(8,12...) fusion(f32[3,258,8,128]{3,2,1,0:T(8,128)S(1)} %constant_dynamic, ...), kind=kLoop, calls=%fused_computation.32 | loop fusion | flops 17436672 | bytes 79011864 | tf_op jit(solution)/shard_map/reduce_sum | solution.py:26
  259.3 1.4 slice_bitcast_fusion.7
  260.7 1.4 slice_bitcast_fusion.4
  262.1 1.5 constant_dynamic-update-slice_fusion.10
  263.6 3.9 %collective-permute-start.2 = (f32[1,256,8,128]{3,2,1,0:T(8,128)}, f32[1,256,8,128]{3,2,1,0:T(8,128)}, u32[]{:S(2)}, u32[]{:S(2)}) collective-permute-start(f32[1,256,8,128]{3,2,1,0:T(8,128)} %get-tuple-element.5), channel_id=1, source_target_pairs={{8,0},{16,8},{24,16},{9,1},{17,9},{25,17},{10,2},{18,10},{26,18},{... | collective-permute-start | bytes 3145736 | tf_op jit(solution)/shard_map/ppermute | solution.py:19
  267.5 3.0 fusion.13
  270.5 1.0 fusion.55
  271.5 5.8 %multiply_reduce_fusion.5 = (f32[258,8,128]{2,1,0:T(8,128)S(1)}, f32[3,258,8,128]{3,2,1,0:T(8,128)S(1)}, f32[3,258,8,128]{3,2,1,0:T(8,128)}, f32[258,8,128]{2,1,...) fusion(f32[3,258,8,128]{3,2,1,0:T(8,128)S(1)} %constant_dynamic-update-slice_fusion, ...), kind=kLoop, calls=%fused_computation.30 | loop fusion | flops 5812224 | bytes 49422344 | tf_op jit(solution)/shard_map/reduce_sum | solution.py:26
  277.5 2.4 slice_bitcast_fusion
  279.9 2.1 slice_bitcast_fusion.2
  282.0 1.5 constant_dynamic-update-slice_fusion.9
  283.5 1.4 constant_dynamic-update-slice_fusion.8
  285.0 1.6 constant_dynamic-update-slice_fusion.7
  286.6 1.4 constant_dynamic-update-slice_fusion.6
  288.1 1.5 constant_dynamic-update-slice_fusion.5
  289.5 1.6 constant_dynamic-update-slice_fusion.4
  291.2 1.5 constant_dynamic-update-slice_fusion.12
  292.6 2.2 collective-permute-start.3
  294.8 2.3 constant_dynamic-update-slice_fusion.3
  297.1 4.9 %fusion.10 = (f32[258,8,128]{2,1,0:T(8,128)S(1)}, f32[258,8,128]{2,1,0:T(8,128)}, f32[258,8,128]{2,1,0:T(8,128)S(1)}, f32[258,8,128]{2,1,0:T(8,128)S(1)}, f32[25...) fusion(f32[258,8,128]{2,1,0:T(8,128)S(1)} %copy-done.4, f32[3,258,8,128]{3,2,1,0:T(8,128)} %get-tuple-element.32, ...), kind=kLoop, calls=%fused_computation.36 | loop fusion | flops 4755456 | bytes 20078592 | tf_op jit(solution)/shard_map/mul | solution.py:28
  302.0 2.6 fusion.52
  304.6 1.0 fusion.49
  305.7 1.0 fusion.46
  306.7 1.0 fusion.43
  307.8 1.0 fusion.40
  308.8 1.0 fusion.37
  309.9 1.0 fusion.34
  310.9 9.5 %collective-permute-done.3 = f32[1,256,8,128]{3,2,1,0:T(8,128)} collective-permute-done((f32[1,256,8,128]{3,2,1,0:T(8,128)}, f32[1,256,8,128]{3,2,1,0:T(8,128)}, u32[]{:S(2)}, u32[]{:S(2)}) %collective-permute-start.3) | collective-permute-done | bytes 1048608 | tf_op jit(solution)/shard_map/ppermute | solution.py:16
  320.4 1.3 constant_dynamic-update-slice_fusion.26
  321.7 1.3 constant_dynamic-update-slice_fusion.25
  323.0 0.2 constant_dynamic-update-slice_fusion.24
  323.2 0.2 constant_dynamic-update-slice_fusion.23
  323.4 0.9 copy-done.7
  324.4 0.3 copy-done.16
  324.6 0.2 constant_dynamic-update-slice_fusion.21
  324.8 0.8 copy-done.11
  325.7 0.2 copy-done.9
  326.1 2.4 constant_dynamic-update-slice_fusion.11
  328.5 10.0 %subtract_divide_fusion = f32[8,256,8,128]{3,2,1,0:T(8,128)} fusion(f32[8,256,8,128]{3,2,1,0:T(8,128)S(1)} %constant_dynamic-update-slice_fusion.19, f32[8,256,8,128]{3,2,1,0:T(8,128)} %constant_dynamic-update-slice_fusion.3, f32[8,256,8,128]{3,2,1,0:T(8,128)} %constant_dynamic-update-slice_fusion.11, f32[8]{0:T(128)S(1)} %subtract_convert_fusion, ...), kind=kLoop, calls=%fused_computation.16 | loop fusion | flops 6291456 | bytes 33554472 | tf_op jit(solution)/shard_map/div | solution.py:66
  (55 shorter events, 0.8 us)
Async XLA Ops:
  7.2 4.5 %copy-start.19 = (s32[32]{0:T(128)S(1)}, s32[32]{0:T(128)}, u32[]{:S(2)}) copy-start(s32[32]{0:T(128)} %param.3) | copy-start | bytes 388
  7.2 223.5 %all-gather.2.cloned.1.call-start = ((), (), s32[]{:S(2)}) async-start(), calls=%async_computation | async-start | bytes 28311552 | tf_op jit(solution)/shard_map/all_gather | solution.py:41
  8.6 13.1 %collective-permute-start.1 = (f32[3,1,8,128]{3,2,1,0:T(8,128)S(1)}, f32[3,1,8,128]{3,2,1,0:T(8,128)S(1)}, u32[]{:S(2)}, u32[]{:S(2)}) collective-permute-start(f32[3,1,8,128]{3,2,1,0:T(8,128)S(1)} %get-tuple-element.56), channel_id=1, source_target_pairs={{1,0},{2,1},{3,2},{4,3},{5,4},{6,5},{7,6},{0,7},{9,8},{10,9},{11,1... | collective-permute-start | bytes 36872 | tf_op jit(solution)/shard_map/ppermute | solution.py:19
  11.7 7.4 %collective-permute-start = (f32[3,1,8,128]{3,2,1,0:T(8,128)S(1)}, f32[3,1,8,128]{3,2,1,0:T(8,128)S(1)}, u32[]{:S(2)}, u32[]{:S(2)}) collective-permute-start(f32[3,1,8,128]{3,2,1,0:T(8,128)S(1)} %get-tuple-element.57), channel_id=1, source_target_pairs={{0,1},{1,2},{2,3},{3,4},{4,5},{5,6},{6,7},{7,0},{8,9},{9,10},{10,1... | collective-permute-start | bytes 36872 | tf_op jit(solution)/shard_map/ppermute | solution.py:16
  259.3 2.8 copy-start.5
  260.7 6.8 %copy-start.3 = (f32[258,8,128]{2,1,0:T(8,128)S(1)}, f32[258,8,128]{2,1,0:T(8,128)}, u32[]{:S(2)}) copy-start(f32[258,8,128]{2,1,0:T(8,128)} %get-tuple-element.33) | copy-start | bytes 3170308
  262.1 22.9 %copy-start.6 = (f32[258,8,128]{2,1,0:T(8,128)}, f32[258,8,128]{2,1,0:T(8,128)S(1)}, u32[]{:S(2)}) copy-start(f32[258,8,128]{2,1,0:T(8,128)S(1)} %slice_bitcast_fusion.4) | copy-start | bytes 3170308
  262.1 9.4 %slice-start = ((s8[6291456]{0:T(1024)(128)(4,1)}), s8[4194304]{0:T(1024)(128)(4,1)S(1)}, s32[]{:S(2)}) async-start(s8[6291456]{0:T(1024)(128)(4,1)} %bitcast.142), calls=%async_computation.1 | async-start | bytes 8388608
  263.6 62.5 %collective-permute-start.2 = (f32[1,256,8,128]{3,2,1,0:T(8,128)}, f32[1,256,8,128]{3,2,1,0:T(8,128)}, u32[]{:S(2)}, u32[]{:S(2)}) collective-permute-start(f32[1,256,8,128]{3,2,1,0:T(8,128)} %get-tuple-element.5), channel_id=1, source_target_pairs={{8,0},{16,8},{24,16},{9,1},{17,9},{25,17},{10,2},{18,10},{26,18},{... | collective-permute-start | bytes 3145736 | tf_op jit(solution)/shard_map/ppermute | solution.py:19
  267.5 4.1 %slice-start.1 = ((s8[6291456]{0:T(1024)(128)(4,1)}), s8[2097152]{0:T(1024)(128)(4,1)S(1)}, s32[]{:S(2)}) async-start(s8[6291456]{0:T(1024)(128)(4,1)} %bitcast.142), calls=%async_computation.2 | async-start | bytes 4194304
  277.4 4.6 %copy-start.17 = (f32[258,8,128]{2,1,0:T(8,128)}, f32[258,8,128]{2,1,0:T(8,128)S(1)}, u32[]{:S(2)}) copy-start(f32[258,8,128]{2,1,0:T(8,128)S(1)} %get-tuple-element.85) | copy-start | bytes 3170308
  277.5 6.1 %copy-start.12 = (f32[258,8,128]{2,1,0:T(8,128)}, f32[258,8,128]{2,1,0:T(8,128)S(1)}, u32[]{:S(2)}) copy-start(f32[258,8,128]{2,1,0:T(8,128)S(1)} %get-tuple-element.84) | copy-start | bytes 3170308
  279.9 9.6 %copy-start.8 = (f32[258,8,128]{2,1,0:T(8,128)}, f32[258,8,128]{2,1,0:T(8,128)S(1)}, u32[]{:S(2)}) copy-start(f32[258,8,128]{2,1,0:T(8,128)S(1)} %get-tuple-element.81) | copy-start | bytes 3170308
  282.0 4.6 %copy-start.15 = (f32[258,8,128]{2,1,0:T(8,128)}, f32[258,8,128]{2,1,0:T(8,128)S(1)}, u32[]{:S(2)}) copy-start(f32[258,8,128]{2,1,0:T(8,128)S(1)} %get-tuple-element.83) | copy-start | bytes 3170308
  282.0 6.0 %copy-start.10 = (f32[258,8,128]{2,1,0:T(8,128)}, f32[258,8,128]{2,1,0:T(8,128)S(1)}, u32[]{:S(2)}) copy-start(f32[258,8,128]{2,1,0:T(8,128)S(1)} %get-tuple-element.82) | copy-start | bytes 3170308
  282.0 3.0 copy-start.2
  283.5 3.1 copy-start.1
  285.0 3.1 copy-start
  288.0 3.1 copy-start.4
  292.6 27.8 %collective-permute-start.3 = (f32[1,256,8,128]{3,2,1,0:T(8,128)}, f32[1,256,8,128]{3,2,1,0:T(8,128)}, u32[]{:S(2)}, u32[]{:S(2)}) collective-permute-start(f32[1,256,8,128]{3,2,1,0:T(8,128)} %get-tuple-element.3), channel_id=1, source_target_pairs={{0,8},{8,16},{16,24},{1,9},{9,17},{17,25},{2,10},{10,18},{18,26},{... | collective-permute-start | bytes 3145736 | tf_op jit(solution)/shard_map/ppermute | solution.py:16
  306.7 2.1 copy-start.14
  309.9 13.2 %copy-start.18 = (f32[258,8,128]{2,1,0:T(8,128)S(1)}, f32[258,8,128]{2,1,0:T(8,128)}, u32[]{:S(2)}) copy-start(f32[258,8,128]{2,1,0:T(8,128)} %copy-done.17) | copy-start | bytes 3170308
  310.9 12.3 %copy-start.13 = (f32[258,8,128]{2,1,0:T(8,128)S(1)}, f32[258,8,128]{2,1,0:T(8,128)}, u32[]{:S(2)}) copy-start(f32[258,8,128]{2,1,0:T(8,128)} %copy-done.12) | copy-start | bytes 3170308
  323.0 1.2 copy-start.7
  323.2 1.4 copy-start.16
  324.3 1.3 copy-start.11
  324.6 1.3 copy-start.9
Sparse Core Ops, SparseCore 0:
  9.6 221.0 all-gather.1
where the time goes:
time: 346 us; the launch traced here: 345 us
  waiting for transfers between devices  219 us (63%)
  other arithmetic  70 us (20%)
  local copies, waits for them, and re-layouts  27.4 us (8%)
  between operations  19.5 us (6%)
  starting transfers between devices  9.15 us (3%)
    all_gather x1, waiting for transfers between devices, body(): whole = lax.all_gather(velocity, 'gx', axis=1, tiled=True)  209 us
    reduce_sum x2, other arithmetic, terms(): squared = jnp.sum(change * change, axis=0)  28.5 us
    unnamed x21, other arithmetic  21.6 us
    div x1, other arithmetic, body(): flux_slope = (above - below) / spread  9.98 us
    ppermute x2, waiting for transfers between devices, with_halo(): lax.ppermute(lax.slice_in_dim(block, block.shape[dim] - width, None, axis...  9.54 us
    mul x2, other arithmetic, terms(): carried = 0.5 * (moved[0] + base[0]) * squared  7.93 us
    squeeze x5, local copies, waits for them, and re-layouts, terms(): flux = change[0] * squared  7.42 us
    unnamed x48, local copies, waits for them, and re-layouts  7.37 us
  transfers between devices with their start and end apart: 5, of which 2 were waited for; matrix products, arithmetic and copies ran while one was open for 14% of the time, Pallas kernels for 0%

commit v1 on v0

v1 whole, which is shorter than its diff:
```python
import jax
import jax.numpy as jnp
from jax import lax
from jax.experimental import pallas as pl
from jax.experimental.pallas import tpu as pltpu
from jax.sharding import PartitionSpec as P

CORES = 2
STEP = 32


def hop(value, axis, pairs):
    return lax.ppermute(value, axis, pairs)


def spread_gather(velocity):
    group = lax.axis_index("sep")
    place = lax.axis_index("gx")
    groups = lax.axis_size("sep")
    count = lax.axis_size("gx")
    chips = count // CORES
    cells = velocity.shape[1]
    part = cells // groups
    half = part // 2
    chip = place // CORES
    core = place % CORES

    def along(value, links):
        pairs = [(a * CORES + c, b * CORES + c) for a, b in links for c in range(CORES)]
        return hop(value, "gx", pairs)

    def across(value, bit):
        return hop(value, "sep", [(s, s ^ bit) for s in range(groups)])

    def partner(value):
        return hop(value, "gx", [(d, d ^ 1) for d in range(count)])

    pair_swap = [(a, a ^ 1) for a in range(chips)]
    mid = [(1, 2), (2, 1)]
    outward = [(1, 0), (2, 3)]
    mine = lax.dynamic_slice_in_dim(velocity, group * part, part, 1)
    first = along(mine, pair_swap)
    inner2 = along(mine, mid)
    outer2 = along(inner2, outward)
    inner3 = along(first, mid)
    outer3 = along(inner3, outward)
    inside = jnp.logical_or(chip == 1, chip == 2)
    second = jnp.where(inside, inner2, outer2)
    third = jnp.where(inside, inner3, outer3)
    low = chip < chips // 2
    near = chip ^ 1
    middle = jnp.where(low, 2, 1)
    far = jnp.where(low, 3, 0)

    pieces = []

    def keep(value, source, offset):
        pieces.append((value, (source * CORES + core) * cells + offset))
        pieces.append((partner(value), (source * CORES + 1 - core) * cells + offset))

    keep(velocity, chip, 0)
    for slot, source in ((first, near), (second, middle), (third, far)):
        by_x = across(slot, 1)
        by_y = across(slot, 2)
        diag_a = across(by_x[:, :half], 2)
        diag_b = across(by_y[:, half:], 1)
        keep(slot, source, group * part)
        keep(by_x, source, (group ^ 1) * part)
        keep(by_y, source, (group ^ 2) * part)
        keep(diag_a, source, (group ^ 3) * part)
        keep(diag_b, source, (group ^ 3) * part + half)
    return pieces


def kernel(scalars, spreads, *refs):
    pieces = refs[:-4]
    slope_ref, transport_ref, field, sems = refs[-4:]
    step = pl.program_id(0)
    total = field.shape[1]
    members = slope_ref.shape[0]
    rows = slope_ref.shape[1]
    fixed = members + 3

    def copies():
        for number, piece in enumerate(pieces):
            planes = piece.shape[1]
            begin = scalars[fixed + number]
            yield pltpu.make_async_copy(
                piece, field.at[:, pl.ds(begin, planes)], sems.at[number]
            )

    @pl.when(step == 0)
    def _():
        for copy in copies():
            copy.start()
        for copy in copies():
            copy.wait()

    origin = scalars[members + 2] + step * rows

    def base_at(x):
        at = (origin + x + total) & (total - 1)
        return at, [field[c, at] for c in range(3)]

    def term(base, at, number):
        there = (at + scalars[number]) & (total - 1)
        moved = [field[c, there] for c in range(3)]
        change = [m - b for m, b in zip(moved, base)]
        squared = change[0] * change[0] + change[1] * change[1] + change[2] * change[2]
        return change[0], squared, moved[0] + base[0]

    def carried_at(x):
        at, base = base_at(x)
        result = []
        for member in range(members):
            _, squared, twice = term(base, at, member + 1)
            result.append(twice * squared)
        return result

    def both_at(x):
        at, base = base_at(x)
        fluxes, carried = [], []
        for member in range(members + 2):
            change, squared, twice = term(base, at, member)
            fluxes.append(change * squared)
            if 0 < member <= members:
                carried.append(twice * squared)
        return fluxes, carried

    def emit(x, fluxes, before, after):
        for member in range(members):
            slope_ref[member, x] = (fluxes[member + 2] - fluxes[member]) * spreads[member]
            transport_ref[member, x] = 0.25 * (after[member] - before[member])

    def body(x, state):
        before, fluxes, now = state[0], state[1], state[2]
        next_fluxes, after = both_at(x + 1)
        emit(x, fluxes, before, after)
        return now, next_fluxes, after

    before = carried_at(-1)
    fluxes, now = both_at(0)
    lax.fori_loop(0, rows, body, (before, fluxes, now), unroll=2)


def body(velocity, distances):
    group = lax.axis_index("sep")
    groups = lax.axis_size("sep")
    place = lax.axis_index("gx")
    cells = velocity.shape[1]
    total = cells * lax.axis_size("gx")
    members = distances.shape[0] // groups
    if groups == 4 and lax.axis_size("gx") == 4 * CORES:
        pieces = spread_gather(velocity)
    else:
        pieces = [(lax.all_gather(velocity, "gx", axis=1, tiled=True), 0)]
    padded = jnp.concatenate([jnp.zeros((1,), jnp.int32), distances, distances[-1:]])
    near = lax.dynamic_slice_in_dim(padded, group * members, members + 2)
    spreads = 1.0 / (near[2:] - near[:-2]).astype(jnp.float32)
    begins = jnp.stack([jnp.asarray(begin, jnp.int32) for _, begin in pieces])
    scalars = jnp.concatenate([near, jnp.stack([place * cells]).astype(jnp.int32), begins])
    shape = (members, cells) + velocity.shape[2:]
    step = min(STEP, cells)
    block = pl.BlockSpec((members, step) + velocity.shape[2:], lambda i: (0, i, 0, 0))
    smem = pl.BlockSpec(memory_space=pltpu.SMEM)
    field = (velocity.shape[0], total) + velocity.shape[2:]
    return pl.pallas_call(
        kernel,
        grid=(cells // step,),
        out_shape=(jax.ShapeDtypeStruct(shape, jnp.float32),) * 2,
        in_specs=[smem, smem] + [pl.BlockSpec(memory_space=pl.ANY)] * len(pieces),
        out_specs=(block, block),
        scratch_shapes=[
            pltpu.VMEM(field, jnp.float32),
            pltpu.SemaphoreType.DMA((len(pieces),)),
        ],
        compiler_params=pltpu.CompilerParams(
            dimension_semantics=("arbitrary",), vmem_limit_bytes=56 << 20
        ),
        name="terms",
    )(scalars, spreads, *[value for value, _ in pieces])


def solution(mesh):
    placed = (P(None, "gx", None, None), P())
    return jax.shard_map(
        body,
        mesh=mesh,
        in_specs=placed,
        out_specs=(P("sep", "gx", None, None), P("sep", "gx", None, None)),
        check_vma=False,
    )
```

time: 346 us -> 148 us (0.43)
  waiting for transfers between devices: 219 us -> 92.7 us
  other arithmetic: 70 us -> 2.61 us
  local copies, waits for them, and re-layouts: 27.4 us -> 7.64 us
  Pallas kernels: 0 us -> 18.7 us
  between operations: 19.5 us -> 1.05 us
  starting transfers between devices: 9.15 us -> 23.5 us
    all_gather x1 -> x0, waiting for transfers between devices: 209 us -> none  [body(): whole = lax.all_gather(velocity, 'gx', axis=1, tiled=True)]
    ppermute x4 -> x33, waiting for transfers between devices: 9.54 us -> 92.7 us  [hop(): return lax.ppermute(value, axis, pairs)]
    reduce_sum x2 -> x0, other arithmetic: 28.5 us -> none  [terms(): squared = jnp.sum(change * change, axis=0)]
    unnamed x21 -> x0, other arithmetic: 21.6 us -> none
    pallas_call x0 -> x1, Pallas kernels: none -> 18.7 us  [body(): pl.pallas_call(kernel, grid=(cells // step,), out_shape=(jax.ShapeDtypeSt...]
    ppermute x4 -> x33, starting transfers between devices: 9.12 us -> 23.5 us  [hop(): return lax.ppermute(value, axis, pairs)]
    div x1, other arithmetic: 9.98 us -> 0.59 us  [body(): spreads = 1.0 / (near[2:] - near[:-2]).astype(jnp.float32)]
    mul x2 -> x0, other arithmetic: 7.93 us -> none  [terms(): carried = 0.5 * (moved[0] + base[0]) * squared]
  transfers between devices with their start and end apart: 5 -> 33, of which waited for: 2 -> 12; matrix products, arithmetic and copies ran while one was open for 14% -> 6% of each run, Pallas kernels for 0% -> 0%
where the time goes in v1:
time: 148 us; the launch traced here: 146 us
  waiting for transfers between devices  92.7 us (63%)
  starting transfers between devices  23.5 us (16%)
  Pallas kernels  18.7 us (13%)
  local copies, waits for them, and re-layouts  7.64 us (5%)
  other arithmetic  2.61 us (2%)
    ppermute x33, waiting for transfers between devices, hop(): return lax.ppermute(value, axis, pairs)  92.7 us
    ppermute x33, starting transfers between devices, hop(): return lax.ppermute(value, axis, pairs)  23.5 us
    pallas_call x1, Pallas kernels, body(): pl.pallas_call(kernel, grid=(cells // step,), out_shape=(jax.ShapeDtypeSt...  18.7 us
  transfers between devices with their start and end apart: 33, of which 12 were waited for; matrix products, arithmetic and copies ran while one was open for 6% of the time, Pallas kernels for 0%

profile of v1, /device:TPU:4, one launch (start us, length us, event | category | flops | bytes accessed | tf_op | source)
XLA Modules:
  0.0 146.1 jit_solution(7286161609305881052)
XLA Ops:
  0.6 1.3 constant_dynamic-slice_fusion
  2.0 1.6 %collective-permute-start.11 = (f32[3,64,8,128]{3,2,1,0:T(8,128)S(1)}, f32[3,64,8,128]{3,2,1,0:T(8,128)}, u32[]{:S(2)}, u32[]{:S(2)}) collective-permute-start(f32[3,64,8,128]{3,2,1,0:T(8,128)S(1)} %constant_dynamic-slice_fusion), channel_id=1, source_target_pairs={{2,4},{3,5},{4,2},{5,3},{10,12},{11,13},{12,10},{13,11},{18,20},{1... | collective-permute-start | bytes 2359304 | tf_op jit(solution)/shard_map/ppermute | solution.py:13
  3.6 3.6 %collective-permute-start.1 = (f32[3,64,8,128]{3,2,1,0:T(8,128)S(1)}, f32[3,64,8,128]{3,2,1,0:T(8,128)}, u32[]{:S(2)}, u32[]{:S(2)}) collective-permute-start(f32[3,64,8,128]{3,2,1,0:T(8,128)S(1)} %constant_dynamic-slice_fusion), channel_id=1, source_target_pairs={{0,2},{1,3},{2,0},{3,1},{4,6},{5,7},{6,4},{7,5},{8,10},{9,11},{10,... | collective-permute-start | bytes 2359304 | tf_op jit(solution)/shard_map/ppermute | solution.py:13
  7.1 1.3 collective-permute-start.12
  8.4 16.1 %collective-permute-done.1.refs_2_ = f32[3,64,8,128]{3,2,1,0:T(8,128)} collective-permute-done((f32[3,64,8,128]{3,2,1,0:T(8,128)S(1)}, f32[3,64,8,128]{3,2,1,0:T(8,128)}, u32[]{:S(2)}, u32[]{:S(2)}) %collective-permute-start.1) | collective-permute-done | bytes 786464 | tf_op jit(solution)/shard_map/ppermute | solution.py:13
  24.5 0.5 collective-permute-start.5
  25.0 1.5 %collective-permute-start.3 = (f32[3,64,8,128]{3,2,1,0:T(8,128)}, f32[3,64,8,128]{3,2,1,0:T(8,128)}, u32[]{:S(2)}, u32[]{:S(2)}) collective-permute-start(f32[3,64,8,128]{3,2,1,0:T(8,128)} %collective-permute-done.1.refs_2_), channel_id=1, source_target_pairs={{0,8},{8,0},{16,24},{24,16},{1,9},{9,1},{17,25},{25,17},{2,10},{10... | collective-permute-start | bytes 2359304 | tf_op jit(solution)/shard_map/ppermute | solution.py:13
  26.5 1.6 %collective-permute-start.22 = (f32[3,64,8,128]{3,2,1,0:T(8,128)}, f32[3,64,8,128]{3,2,1,0:T(8,128)}, u32[]{:S(2)}, u32[]{:S(2)}) collective-permute-start(f32[3,64,8,128]{3,2,1,0:T(8,128)} %collective-permute-done.1.refs_2_), channel_id=1, source_target_pairs={{2,4},{3,5},{4,2},{5,3},{10,12},{11,13},{12,10},{13,11},{18,20},{1... | collective-permute-start | bytes 2359304 | tf_op jit(solution)/shard_map/ppermute | solution.py:13
  28.1 15.1 %collective-permute-done.12 = f32[3,64,8,128]{3,2,1,0:T(8,128)} collective-permute-done((f32[3,64,8,128]{3,2,1,0:T(8,128)}, f32[3,64,8,128]{3,2,1,0:T(8,128)}, u32[]{:S(2)}, u32[]{:S(2)}) %collective-permute-start.12) | collective-permute-done | bytes 786464 | tf_op jit(solution)/shard_map/ppermute | solution.py:13
  43.1 1.2 broadcast_select_fusion.1.refs_12_
  44.3 0.6 collective-permute-start.16
  44.9 1.0 slice.37
  46.0 1.6 %collective-permute-start.9 = (f32[3,32,8,128]{3,2,1,0:T(8,128)S(1)}, f32[3,32,8,128]{3,2,1,0:T(8,128)S(1)}, u32[]{:S(2)}, u32[]{:S(2)}) collective-permute-start(f32[3,32,8,128]{3,2,1,0:T(8,128)S(1)} %slice.37), channel_id=1, source_target_pairs={{0,8},{8,0},{16,24},{24,16},{1,9},{9,1},{17,25},{25,17},{2,10},{10... | collective-permute-start | bytes 1179656 | tf_op jit(solution)/shard_map/ppermute | solution.py:13
  47.5 0.5 collective-permute-start.14
  48.1 1.0 slice.36
  49.2 1.6 %collective-permute-start.7 = (f32[3,32,8,128]{3,2,1,0:T(8,128)S(1)}, f32[3,32,8,128]{3,2,1,0:T(8,128)S(1)}, u32[]{:S(2)}, u32[]{:S(2)}) collective-permute-start(f32[3,32,8,128]{3,2,1,0:T(8,128)S(1)} %slice.36), channel_id=1, source_target_pairs={{0,16},{8,24},{16,0},{24,8},{1,17},{9,25},{17,1},{25,9},{2,18},{10... | collective-permute-start | bytes 1179656 | tf_op jit(solution)/shard_map/ppermute | solution.py:13
  50.8 7.2 %collective-permute-done.9.refs_10_ = f32[3,32,8,128]{3,2,1,0:T(8,128)S(1)} collective-permute-done((f32[3,32,8,128]{3,2,1,0:T(8,128)S(1)}, f32[3,32,8,128]{3,2,1,0:T(8,128)S(1)}, u32[]{:S(2)}, u32[]{:S(2)}) %collective-permute-start.9) | collective-permute-done | bytes 393248 | tf_op jit(solution)/shard_map/ppermute | solution.py:13
  58.0 1.3 collective-permute-start.23
  59.3 11.4 %collective-permute-done.7.refs_8_ = f32[3,32,8,128]{3,2,1,0:T(8,128)S(1)} collective-permute-done((f32[3,32,8,128]{3,2,1,0:T(8,128)S(1)}, f32[3,32,8,128]{3,2,1,0:T(8,128)S(1)}, u32[]{:S(2)}, u32[]{:S(2)}) %collective-permute-start.7) | collective-permute-done | bytes 393248 | tf_op jit(solution)/shard_map/ppermute | solution.py:13
  70.7 0.5 collective-permute-start.6
  71.2 0.8 collective-permute-done.14.refs_14_
  72.0 0.5 collective-permute-start.4
  72.6 1.4 collective-permute-done.23
  74.0 4.1 %collective-permute-done.10.refs_11_ = f32[3,32,8,128]{3,2,1,0:T(8,128)S(1)} collective-permute-done((f32[3,32,8,128]{3,2,1,0:T(8,128)S(1)}, f32[3,32,8,128]{3,2,1,0:T(8,128)S(1)}, u32[]{:S(2)}, u32[]{:S(2)}) %collective-permute-start.10) | collective-permute-done | bytes 393248 | tf_op jit(solution)/shard_map/ppermute | solution.py:13
  78.0 0.7 copy-done.13
  78.8 1.5 %collective-permute-start.20 = (f32[3,32,8,128]{3,2,1,0:T(8,128)S(1)}, f32[3,32,8,128]{3,2,1,0:T(8,128)S(1)}, u32[]{:S(2)}, u32[]{:S(2)}) collective-permute-start(f32[3,32,8,128]{3,2,1,0:T(8,128)S(1)} %slice.39), channel_id=1, source_target_pairs={{0,8},{8,0},{16,24},{24,16},{1,9},{9,1},{17,25},{25,17},{2,10},{10... | collective-permute-start | bytes 1179656 | tf_op jit(solution)/shard_map/ppermute | solution.py:13
  80.3 0.1 broadcast_select_fusion.refs_22_
  80.4 0.6 collective-permute-start.27
  81.0 1.6 %collective-permute-start.18 = (f32[3,32,8,128]{3,2,1,0:T(8,128)S(1)}, f32[3,32,8,128]{3,2,1,0:T(8,128)S(1)}, u32[]{:S(2)}, u32[]{:S(2)}) collective-permute-start(f32[3,32,8,128]{3,2,1,0:T(8,128)S(1)} %slice.38), channel_id=1, source_target_pairs={{0,16},{8,24},{16,0},{24,8},{1,17},{9,25},{17,1},{25,9},{2,18},{10... | collective-permute-start | bytes 1179656 | tf_op jit(solution)/shard_map/ppermute | solution.py:13
  82.6 0.5 collective-permute-start.25
  83.1 7.6 %collective-permute-done.20.refs_20_ = f32[3,32,8,128]{3,2,1,0:T(8,128)S(1)} collective-permute-done((f32[3,32,8,128]{3,2,1,0:T(8,128)S(1)}, f32[3,32,8,128]{3,2,1,0:T(8,128)S(1)}, u32[]{:S(2)}, u32[]{:S(2)}) %collective-permute-start.20) | collective-permute-done | bytes 393248 | tf_op jit(solution)/shard_map/ppermute | solution.py:13
  90.8 17.4 %collective-permute-done.18.refs_18_ = f32[3,32,8,128]{3,2,1,0:T(8,128)S(1)} collective-permute-done((f32[3,32,8,128]{3,2,1,0:T(8,128)S(1)}, f32[3,32,8,128]{3,2,1,0:T(8,128)S(1)}, u32[]{:S(2)}, u32[]{:S(2)}) %collective-permute-start.18) | collective-permute-done | bytes 393248 | tf_op jit(solution)/shard_map/ppermute | solution.py:13
  108.2 0.5 collective-permute-start.15
  108.7 0.1 collective-permute-start.24
  108.8 0.4 collective-permute-start.19
  109.2 1.0 slice.41
  110.3 1.0 slice.40
  111.3 0.6 collective-permute-start.31
  111.9 1.4 collective-permute-done.19.refs_19_
  113.3 0.5 collective-permute-start.29
  113.8 0.5 collective-permute-start.26
  114.4 8.2 %collective-permute-done.31.refs_30_ = f32[3,32,8,128]{3,2,1,0:T(8,128)} collective-permute-done((f32[3,32,8,128]{3,2,1,0:T(8,128)S(1)}, f32[3,32,8,128]{3,2,1,0:T(8,128)}, u32[]{:S(2)}, u32[]{:S(2)}) %collective-permute-start.31) | collective-permute-done | bytes 393248 | tf_op jit(solution)/shard_map/ppermute | solution.py:13
  122.6 2.0 %collective-permute-done.29.refs_28_ = f32[3,32,8,128]{3,2,1,0:T(8,128)} collective-permute-done((f32[3,32,8,128]{3,2,1,0:T(8,128)S(1)}, f32[3,32,8,128]{3,2,1,0:T(8,128)}, u32[]{:S(2)}, u32[]{:S(2)}) %collective-permute-start.29) | collective-permute-done | bytes 393248 | tf_op jit(solution)/shard_map/ppermute | solution.py:13
  124.8 0.6 slice.27
  125.3 0.7 pad_add_fusion
  126.1 0.7 concatenate.7.scalars
  126.8 0.6 convert_divide_fusion.spreads
  127.4 18.7 %terms.1 = (f32[8,256,8,128]{3,2,1,0:T(8,128)}, f32[8,256,8,128]{3,2,1,0:T(8,128)}) custom-call(s32[43]{0:T(128)} %concatenate.7.scalars, f32[8]{0:T(128)} %convert_divide_fusion.spreads, f32[3,256,8,128]{3,2,1,0:T(8,128)} %refs_0_.1, f32[3,256,8,128]{3,2,1,0:T(8,128)} %collective-permute-done.refs_1_, f32[3,64,8,128]{3,2,1,0:T(8,128)} %collective-permute-done.1.refs_2_, ...), custom_call_target="tpu_custom_call" | custom-call | tf_op jit(solution)/shard_map/terms/pallas_call | solution.py:167
  (73 shorter events, 0.4 us)
Async XLA Ops:
  0.6 70.1 %copy-start = (f32[3,256,8,128]{3,2,1,0:T(8,128)S(1)}, f32[3,256,8,128]{3,2,1,0:T(8,128)}, u32[]{:S(2)}) copy-start(f32[3,256,8,128]{3,2,1,0:T(8,128)} %refs_0_.1) | copy-start | bytes 9437188
  2.0 5.1 %collective-permute-start.11 = (f32[3,64,8,128]{3,2,1,0:T(8,128)S(1)}, f32[3,64,8,128]{3,2,1,0:T(8,128)}, u32[]{:S(2)}, u32[]{:S(2)}) collective-permute-start(f32[3,64,8,128]{3,2,1,0:T(8,128)S(1)} %constant_dynamic-slice_fusion), channel_id=1, source_target_pairs={{2,4},{3,5},{4,2},{5,3},{10,12},{11,13},{12,10},{13,11},{18,20},{1... | collective-permute-start | bytes 2359304 | tf_op jit(solution)/shard_map/ppermute | solution.py:13
  3.6 20.9 %collective-permute-start.1 = (f32[3,64,8,128]{3,2,1,0:T(8,128)S(1)}, f32[3,64,8,128]{3,2,1,0:T(8,128)}, u32[]{:S(2)}, u32[]{:S(2)}) collective-permute-start(f32[3,64,8,128]{3,2,1,0:T(8,128)S(1)} %constant_dynamic-slice_fusion), channel_id=1, source_target_pairs={{0,2},{1,3},{2,0},{3,1},{4,6},{5,7},{6,4},{7,5},{8,10},{9,11},{10,... | collective-permute-start | bytes 2359304 | tf_op jit(solution)/shard_map/ppermute | solution.py:13
  7.1 36.0 %collective-permute-start.12 = (f32[3,64,8,128]{3,2,1,0:T(8,128)}, f32[3,64,8,128]{3,2,1,0:T(8,128)}, u32[]{:S(2)}, u32[]{:S(2)}) collective-permute-start(f32[3,64,8,128]{3,2,1,0:T(8,128)} %collective-permute-done.11), channel_id=1, source_target_pairs={{2,0},{3,1},{4,6},{5,7},{10,8},{11,9},{12,14},{13,15},{18,16},{19,... | collective-permute-start | bytes 2359304 | tf_op jit(solution)/shard_map/ppermute | solution.py:13
  24.5 20.4 %collective-permute-start.5 = (f32[3,64,8,128]{3,2,1,0:T(8,128)}, f32[3,64,8,128]{3,2,1,0:T(8,128)}, u32[]{:S(2)}, u32[]{:S(2)}) collective-permute-start(f32[3,64,8,128]{3,2,1,0:T(8,128)} %collective-permute-done.1.refs_2_), channel_id=1, source_target_pairs={{0,16},{8,24},{16,0},{24,8},{1,17},{9,25},{17,1},{25,9},{2,18},{10... | collective-permute-start | bytes 2359304 | tf_op jit(solution)/shard_map/ppermute | solution.py:13
  25.0 22.5 %collective-permute-start.3 = (f32[3,64,8,128]{3,2,1,0:T(8,128)}, f32[3,64,8,128]{3,2,1,0:T(8,128)}, u32[]{:S(2)}, u32[]{:S(2)}) collective-permute-start(f32[3,64,8,128]{3,2,1,0:T(8,128)} %collective-permute-done.1.refs_2_), channel_id=1, source_target_pairs={{0,8},{8,0},{16,24},{24,16},{1,9},{9,1},{17,25},{25,17},{2,10},{10... | collective-permute-start | bytes 2359304 | tf_op jit(solution)/shard_map/ppermute | solution.py:13
  26.5 22.6 %collective-permute-start.22 = (f32[3,64,8,128]{3,2,1,0:T(8,128)}, f32[3,64,8,128]{3,2,1,0:T(8,128)}, u32[]{:S(2)}, u32[]{:S(2)}) collective-permute-start(f32[3,64,8,128]{3,2,1,0:T(8,128)} %collective-permute-done.1.refs_2_), channel_id=1, source_target_pairs={{2,4},{3,5},{4,2},{5,3},{10,12},{11,13},{12,10},{13,11},{18,20},{1... | collective-permute-start | bytes 2359304 | tf_op jit(solution)/shard_map/ppermute | solution.py:13
  28.0 21.1 %collective-permute-start.2 = (f32[3,64,8,128]{3,2,1,0:T(8,128)}, f32[3,64,8,128]{3,2,1,0:T(8,128)}, u32[]{:S(2)}, u32[]{:S(2)}) collective-permute-start(f32[3,64,8,128]{3,2,1,0:T(8,128)} %collective-permute-done.1.refs_2_), channel_id=1, source_target_pairs={{0,1},{1,0},{2,3},{3,2},{4,5},{5,4},{6,7},{7,6},{8,9},{9,8},{10,11... | collective-permute-start | bytes 2359304 | tf_op jit(solution)/shard_map/ppermute | solution.py:13
  44.3 65.9 %copy-start.1 = (f32[3,64,8,128]{3,2,1,0:T(8,128)}, f32[3,64,8,128]{3,2,1,0:T(8,128)S(1)}, u32[]{:S(2)}) copy-start(f32[3,64,8,128]{3,2,1,0:T(8,128)S(1)} %broadcast_select_fusion.1.refs_12_) | copy-start | bytes 2359300
  44.3 26.4 %collective-permute-start.16 = (f32[3,64,8,128]{3,2,1,0:T(8,128)S(1)}, f32[3,64,8,128]{3,2,1,0:T(8,128)S(1)}, u32[]{:S(2)}, u32[]{:S(2)}) collective-permute-start(f32[3,64,8,128]{3,2,1,0:T(8,128)S(1)} %broadcast_select_fusion.1.refs_12_), channel_id=1, source_target_pairs={{0,16},{8,24},{16,0},{24,8},{1,17},{9,25},{17,1},{25,9},{2,18},{10... | collective-permute-start | bytes 2359304 | tf_op jit(solution)/shard_map/ppermute | solution.py:13
  45.9 78.8 %copy-start.19 = (s32[32]{0:T(128)S(1)}, s32[32]{0:T(128)}, u32[]{:S(2)}) copy-start(s32[32]{0:T(128)} %param.3) | copy-start | bytes 388
  46.0 12.1 %collective-permute-start.9 = (f32[3,32,8,128]{3,2,1,0:T(8,128)S(1)}, f32[3,32,8,128]{3,2,1,0:T(8,128)S(1)}, u32[]{:S(2)}, u32[]{:S(2)}) collective-permute-start(f32[3,32,8,128]{3,2,1,0:T(8,128)S(1)} %slice.37), channel_id=1, source_target_pairs={{0,8},{8,0},{16,24},{24,16},{1,9},{9,1},{17,25},{25,17},{2,10},{10... | collective-permute-start | bytes 1179656 | tf_op jit(solution)/shard_map/ppermute | solution.py:13
  47.5 24.5 %collective-permute-start.14 = (f32[3,64,8,128]{3,2,1,0:T(8,128)S(1)}, f32[3,64,8,128]{3,2,1,0:T(8,128)S(1)}, u32[]{:S(2)}, u32[]{:S(2)}) collective-permute-start(f32[3,64,8,128]{3,2,1,0:T(8,128)S(1)} %broadcast_select_fusion.1.refs_12_), channel_id=1, source_target_pairs={{0,8},{8,0},{16,24},{24,16},{1,9},{9,1},{17,25},{25,17},{2,10},{10... | collective-permute-start | bytes 2359304 | tf_op jit(solution)/shard_map/ppermute | solution.py:13
  49.1 22.9 %collective-permute-start.13 = (f32[3,64,8,128]{3,2,1,0:T(8,128)S(1)}, f32[3,64,8,128]{3,2,1,0:T(8,128)S(1)}, u32[]{:S(2)}, u32[]{:S(2)}) collective-permute-start(f32[3,64,8,128]{3,2,1,0:T(8,128)S(1)} %broadcast_select_fusion.1.refs_12_), channel_id=1, source_target_pairs={{0,1},{1,0},{2,3},{3,2},{4,5},{5,4},{6,7},{7,6},{8,9},{9,8},{10,11... | collective-permute-start | bytes 2359304 | tf_op jit(solution)/shard_map/ppermute | solution.py:13
  49.2 21.5 %collective-permute-start.7 = (f32[3,32,8,128]{3,2,1,0:T(8,128)S(1)}, f32[3,32,8,128]{3,2,1,0:T(8,128)S(1)}, u32[]{:S(2)}, u32[]{:S(2)}) collective-permute-start(f32[3,32,8,128]{3,2,1,0:T(8,128)S(1)} %slice.36), channel_id=1, source_target_pairs={{0,16},{8,24},{16,0},{24,8},{1,17},{9,25},{17,1},{25,9},{2,18},{10... | collective-permute-start | bytes 1179656 | tf_op jit(solution)/shard_map/ppermute | solution.py:13
  58.0 69.4 %copy-start.11 = (f32[3,32,8,128]{3,2,1,0:T(8,128)}, f32[3,32,8,128]{3,2,1,0:T(8,128)S(1)}, u32[]{:S(2)}) copy-start(f32[3,32,8,128]{3,2,1,0:T(8,128)S(1)} %collective-permute-done.9.refs_10_) | copy-start | bytes 1179652
  58.0 16.0 %collective-permute-start.23 = (f32[3,64,8,128]{3,2,1,0:T(8,128)}, f32[3,64,8,128]{3,2,1,0:T(8,128)S(1)}, u32[]{:S(2)}, u32[]{:S(2)}) collective-permute-start(f32[3,64,8,128]{3,2,1,0:T(8,128)} %collective-permute-done.22), channel_id=1, source_target_pairs={{2,0},{3,1},{4,6},{5,7},{10,8},{11,9},{12,14},{13,15},{18,16},{19,... | collective-permute-start | bytes 2359304 | tf_op jit(solution)/shard_map/ppermute | solution.py:13
  70.7 53.9 %copy-start.12 = (f32[3,32,8,128]{3,2,1,0:T(8,128)}, f32[3,32,8,128]{3,2,1,0:T(8,128)S(1)}, u32[]{:S(2)}) copy-start(f32[3,32,8,128]{3,2,1,0:T(8,128)S(1)} %collective-permute-done.7.refs_8_) | copy-start | bytes 1179652
  70.7 56.7 %collective-permute-start = (f32[3,256,8,128]{3,2,1,0:T(8,128)S(1)}, f32[3,256,8,128]{3,2,1,0:T(8,128)}, u32[]{:S(2)}, u32[]{:S(2)}) collective-permute-start(f32[3,256,8,128]{3,2,1,0:T(8,128)S(1)} %copy-done), channel_id=1, source_target_pairs={{0,1},{1,0},{2,3},{3,2},{4,5},{5,4},{6,7},{7,6},{8,9},{9,8},{10,11... | collective-permute-start | bytes 9437192 | tf_op jit(solution)/shard_map/ppermute | solution.py:13
  70.7 43.1 %copy-start.3 = (f32[3,64,8,128]{3,2,1,0:T(8,128)}, f32[3,64,8,128]{3,2,1,0:T(8,128)S(1)}, u32[]{:S(2)}) copy-start(f32[3,64,8,128]{3,2,1,0:T(8,128)S(1)} %collective-permute-done.16.refs_16_) | copy-start | bytes 2359300
  70.7 9.7 %collective-permute-start.6 = (f32[3,64,8,128]{3,2,1,0:T(8,128)}, f32[3,64,8,128]{3,2,1,0:T(8,128)S(1)}, u32[]{:S(2)}, u32[]{:S(2)}) collective-permute-start(f32[3,64,8,128]{3,2,1,0:T(8,128)} %collective-permute-done.5.refs_6_), channel_id=1, source_target_pairs={{0,1},{1,0},{2,3},{3,2},{4,5},{5,4},{6,7},{7,6},{8,9},{9,8},{10,11... | collective-permute-start | bytes 2359304 | tf_op jit(solution)/shard_map/ppermute | solution.py:13
  72.0 42.4 %copy-start.4 = (f32[3,64,8,128]{3,2,1,0:T(8,128)}, f32[3,64,8,128]{3,2,1,0:T(8,128)S(1)}, u32[]{:S(2)}) copy-start(f32[3,64,8,128]{3,2,1,0:T(8,128)S(1)} %collective-permute-done.14.refs_14_) | copy-start | bytes 2359300
  72.0 6.0 %collective-permute-start.10 = (f32[3,32,8,128]{3,2,1,0:T(8,128)S(1)}, f32[3,32,8,128]{3,2,1,0:T(8,128)S(1)}, u32[]{:S(2)}, u32[]{:S(2)}) collective-permute-start(f32[3,32,8,128]{3,2,1,0:T(8,128)S(1)} %collective-permute-done.9.refs_10_), channel_id=1, source_target_pairs={{0,1},{1,0},{2,3},{3,2},{4,5},{5,4},{6,7},{7,6},{8,9},{9,8},{10,11... | collective-permute-start | bytes 1179656 | tf_op jit(solution)/shard_map/ppermute | solution.py:13
  72.0 10.6 %collective-permute-start.4 = (f32[3,64,8,128]{3,2,1,0:T(8,128)}, f32[3,64,8,128]{3,2,1,0:T(8,128)S(1)}, u32[]{:S(2)}, u32[]{:S(2)}) collective-permute-start(f32[3,64,8,128]{3,2,1,0:T(8,128)} %collective-permute-done.3.refs_4_), channel_id=1, source_target_pairs={{0,1},{1,0},{2,3},{3,2},{4,5},{5,4},{6,7},{7,6},{8,9},{9,8},{10,11... | collective-permute-start | bytes 2359304 | tf_op jit(solution)/shard_map/ppermute | solution.py:13
  74.0 7.0 %collective-permute-start.8 = (f32[3,32,8,128]{3,2,1,0:T(8,128)S(1)}, f32[3,32,8,128]{3,2,1,0:T(8,128)S(1)}, u32[]{:S(2)}, u32[]{:S(2)}) collective-permute-start(f32[3,32,8,128]{3,2,1,0:T(8,128)S(1)} %collective-permute-done.7.refs_8_), channel_id=1, source_target_pairs={{0,1},{1,0},{2,3},{3,2},{4,5},{5,4},{6,7},{7,6},{8,9},{9,8},{10,11... | collective-permute-start | bytes 1179656 | tf_op jit(solution)/shard_map/ppermute | solution.py:13
  78.8 12.0 %collective-permute-start.20 = (f32[3,32,8,128]{3,2,1,0:T(8,128)S(1)}, f32[3,32,8,128]{3,2,1,0:T(8,128)S(1)}, u32[]{:S(2)}, u32[]{:S(2)}) collective-permute-start(f32[3,32,8,128]{3,2,1,0:T(8,128)S(1)} %slice.39), channel_id=1, source_target_pairs={{0,8},{8,0},{16,24},{24,16},{1,9},{9,1},{17,25},{25,17},{2,10},{10... | collective-permute-start | bytes 1179656 | tf_op jit(solution)/shard_map/ppermute | solution.py:13
  80.4 30.9 %copy-start.2 = (f32[3,64,8,128]{3,2,1,0:T(8,128)}, f32[3,64,8,128]{3,2,1,0:T(8,128)S(1)}, u32[]{:S(2)}) copy-start(f32[3,64,8,128]{3,2,1,0:T(8,128)S(1)} %broadcast_select_fusion.refs_22_) | copy-start | bytes 2359300
  80.4 42.2 %copy-start.6 = (f32[3,64,8,128]{3,2,1,0:T(8,128)}, f32[3,64,8,128]{3,2,1,0:T(8,128)S(1)}, u32[]{:S(2)}) copy-start(f32[3,64,8,128]{3,2,1,0:T(8,128)S(1)} %collective-permute-done.6.refs_7_) | copy-start | bytes 2359300
  80.4 28.3 %collective-permute-start.27 = (f32[3,64,8,128]{3,2,1,0:T(8,128)S(1)}, f32[3,64,8,128]{3,2,1,0:T(8,128)}, u32[]{:S(2)}, u32[]{:S(2)}) collective-permute-start(f32[3,64,8,128]{3,2,1,0:T(8,128)S(1)} %broadcast_select_fusion.refs_22_), channel_id=1, source_target_pairs={{0,16},{8,24},{16,0},{24,8},{1,17},{9,25},{17,1},{25,9},{2,18},{10... | collective-permute-start | bytes 2359304 | tf_op jit(solution)/shard_map/ppermute | solution.py:13
  81.0 43.6 %copy-start.14 = (f32[3,32,8,128]{3,2,1,0:T(8,128)}, f32[3,32,8,128]{3,2,1,0:T(8,128)S(1)}, u32[]{:S(2)}) copy-start(f32[3,32,8,128]{3,2,1,0:T(8,128)S(1)} %collective-permute-done.8.refs_9_) | copy-start | bytes 1179652
  81.0 27.2 %collective-permute-start.18 = (f32[3,32,8,128]{3,2,1,0:T(8,128)S(1)}, f32[3,32,8,128]{3,2,1,0:T(8,128)S(1)}, u32[]{:S(2)}, u32[]{:S(2)}) collective-permute-start(f32[3,32,8,128]{3,2,1,0:T(8,128)S(1)} %slice.38), channel_id=1, source_target_pairs={{0,16},{8,24},{16,0},{24,8},{1,17},{9,25},{17,1},{25,9},{2,18},{10... | collective-permute-start | bytes 1179656 | tf_op jit(solution)/shard_map/ppermute | solution.py:13
  82.6 40.0 %copy-start.7 = (f32[3,64,8,128]{3,2,1,0:T(8,128)}, f32[3,64,8,128]{3,2,1,0:T(8,128)S(1)}, u32[]{:S(2)}) copy-start(f32[3,64,8,128]{3,2,1,0:T(8,128)S(1)} %collective-permute-done.4.refs_5_) | copy-start | bytes 2359300
  82.6 26.2 %collective-permute-start.25 = (f32[3,64,8,128]{3,2,1,0:T(8,128)S(1)}, f32[3,64,8,128]{3,2,1,0:T(8,128)}, u32[]{:S(2)}, u32[]{:S(2)}) collective-permute-start(f32[3,64,8,128]{3,2,1,0:T(8,128)S(1)} %broadcast_select_fusion.refs_22_), channel_id=1, source_target_pairs={{0,8},{8,0},{16,24},{24,16},{1,9},{9,1},{17,25},{25,17},{2,10},{10... | collective-permute-start | bytes 2359304 | tf_op jit(solution)/shard_map/ppermute | solution.py:13
  90.8 33.8 %copy-start.15 = (f32[3,32,8,128]{3,2,1,0:T(8,128)}, f32[3,32,8,128]{3,2,1,0:T(8,128)S(1)}, u32[]{:S(2)}) copy-start(f32[3,32,8,128]{3,2,1,0:T(8,128)S(1)} %collective-permute-done.20.refs_20_) | copy-start | bytes 1179652
  90.8 17.4 %collective-permute-start.21 = (f32[3,32,8,128]{3,2,1,0:T(8,128)S(1)}, f32[3,32,8,128]{3,2,1,0:T(8,128)S(1)}, u32[]{:S(2)}, u32[]{:S(2)}) collective-permute-start(f32[3,32,8,128]{3,2,1,0:T(8,128)S(1)} %collective-permute-done.20.refs_20_), channel_id=1, source_target_pairs={{0,1},{1,0},{2,3},{3,2},{4,5},{5,4},{6,7},{7,6},{8,9},{9,8},{10,11... | collective-permute-start | bytes 1179656 | tf_op jit(solution)/shard_map/ppermute | solution.py:13
  108.2 16.4 %copy-start.16 = (f32[3,32,8,128]{3,2,1,0:T(8,128)}, f32[3,32,8,128]{3,2,1,0:T(8,128)S(1)}, u32[]{:S(2)}) copy-start(f32[3,32,8,128]{3,2,1,0:T(8,128)S(1)} %collective-permute-done.18.refs_18_) | copy-start | bytes 1179652
  108.2 3.1 %collective-permute-start.17 = (f32[3,64,8,128]{3,2,1,0:T(8,128)S(1)}, f32[3,64,8,128]{3,2,1,0:T(8,128)S(1)}, u32[]{:S(2)}, u32[]{:S(2)}) collective-permute-start(f32[3,64,8,128]{3,2,1,0:T(8,128)S(1)} %collective-permute-done.16.refs_16_), channel_id=1, source_target_pairs={{0,1},{1,0},{2,3},{3,2},{4,5},{5,4},{6,7},{7,6},{8,9},{9,8},{10,11... | collective-permute-start | bytes 2359304 | tf_op jit(solution)/shard_map/ppermute | solution.py:13
  108.2 16.4 %copy-start.17 = (f32[3,32,8,128]{3,2,1,0:T(8,128)}, f32[3,32,8,128]{3,2,1,0:T(8,128)S(1)}, u32[]{:S(2)}) copy-start(f32[3,32,8,128]{3,2,1,0:T(8,128)S(1)} %collective-permute-done.21.refs_21_) | copy-start | bytes 1179652
  108.2 5.6 %collective-permute-start.15 = (f32[3,64,8,128]{3,2,1,0:T(8,128)S(1)}, f32[3,64,8,128]{3,2,1,0:T(8,128)S(1)}, u32[]{:S(2)}, u32[]{:S(2)}) collective-permute-start(f32[3,64,8,128]{3,2,1,0:T(8,128)S(1)} %collective-permute-done.14.refs_14_), channel_id=1, source_target_pairs={{0,1},{1,0},{2,3},{3,2},{4,5},{5,4},{6,7},{7,6},{8,9},{9,8},{10,11... | collective-permute-start | bytes 2359304 | tf_op jit(solution)/shard_map/ppermute | solution.py:13
  108.7 5.1 %collective-permute-start.24 = (f32[3,64,8,128]{3,2,1,0:T(8,128)S(1)}, f32[3,64,8,128]{3,2,1,0:T(8,128)S(1)}, u32[]{:S(2)}, u32[]{:S(2)}) collective-permute-start(f32[3,64,8,128]{3,2,1,0:T(8,128)S(1)} %broadcast_select_fusion.refs_22_), channel_id=1, source_target_pairs={{0,1},{1,0},{2,3},{3,2},{4,5},{5,4},{6,7},{7,6},{8,9},{9,8},{10,11... | collective-permute-start | bytes 2359304 | tf_op jit(solution)/shard_map/ppermute | solution.py:13
  108.8 4.5 %collective-permute-start.19 = (f32[3,32,8,128]{3,2,1,0:T(8,128)S(1)}, f32[3,32,8,128]{3,2,1,0:T(8,128)S(1)}, u32[]{:S(2)}, u32[]{:S(2)}) collective-permute-start(f32[3,32,8,128]{3,2,1,0:T(8,128)S(1)} %collective-permute-done.18.refs_18_), channel_id=1, source_target_pairs={{0,1},{1,0},{2,3},{3,2},{4,5},{5,4},{6,7},{7,6},{8,9},{9,8},{10,11... | collective-permute-start | bytes 1179656 | tf_op jit(solution)/shard_map/ppermute | solution.py:13
  111.3 13.3 %copy-start.8 = (f32[3,64,8,128]{3,2,1,0:T(8,128)}, f32[3,64,8,128]{3,2,1,0:T(8,128)S(1)}, u32[]{:S(2)}) copy-start(f32[3,64,8,128]{3,2,1,0:T(8,128)S(1)} %collective-permute-done.17.refs_17_) | copy-start | bytes 2359300
  111.3 11.3 %collective-permute-start.31 = (f32[3,32,8,128]{3,2,1,0:T(8,128)S(1)}, f32[3,32,8,128]{3,2,1,0:T(8,128)}, u32[]{:S(2)}, u32[]{:S(2)}) collective-permute-start(f32[3,32,8,128]{3,2,1,0:T(8,128)S(1)} %slice.41), channel_id=1, source_target_pairs={{0,8},{8,0},{16,24},{24,16},{1,9},{9,1},{17,25},{25,17},{2,10},{10... | collective-permute-start | bytes 1179656 | tf_op jit(solution)/shard_map/ppermute | solution.py:13
  113.3 11.3 %collective-permute-start.29 = (f32[3,32,8,128]{3,2,1,0:T(8,128)S(1)}, f32[3,32,8,128]{3,2,1,0:T(8,128)}, u32[]{:S(2)}, u32[]{:S(2)}) collective-permute-start(f32[3,32,8,128]{3,2,1,0:T(8,128)S(1)} %slice.40), channel_id=1, source_target_pairs={{0,16},{8,24},{16,0},{24,8},{1,17},{9,25},{17,1},{25,9},{2,18},{10... | collective-permute-start | bytes 1179656 | tf_op jit(solution)/shard_map/ppermute | solution.py:13
  113.8 13.6 %collective-permute-start.28 = (f32[3,64,8,128]{3,2,1,0:T(8,128)}, f32[3,64,8,128]{3,2,1,0:T(8,128)}, u32[]{:S(2)}, u32[]{:S(2)}) collective-permute-start(f32[3,64,8,128]{3,2,1,0:T(8,128)} %collective-permute-done.27.refs_26_), channel_id=1, source_target_pairs={{0,1},{1,0},{2,3},{3,2},{4,5},{5,4},{6,7},{7,6},{8,9},{9,8},{10,11... | collective-permute-start | bytes 2359304 | tf_op jit(solution)/shard_map/ppermute | solution.py:13
  113.8 13.6 %collective-permute-start.26 = (f32[3,64,8,128]{3,2,1,0:T(8,128)}, f32[3,64,8,128]{3,2,1,0:T(8,128)}, u32[]{:S(2)}, u32[]{:S(2)}) collective-permute-start(f32[3,64,8,128]{3,2,1,0:T(8,128)} %collective-permute-done.25.refs_24_), channel_id=1, source_target_pairs={{0,1},{1,0},{2,3},{3,2},{4,5},{5,4},{6,7},{7,6},{8,9},{9,8},{10,11... | collective-permute-start | bytes 2359304 | tf_op jit(solution)/shard_map/ppermute | solution.py:13
  122.6 4.8 %collective-permute-start.32 = (f32[3,32,8,128]{3,2,1,0:T(8,128)}, f32[3,32,8,128]{3,2,1,0:T(8,128)}, u32[]{:S(2)}, u32[]{:S(2)}) collective-permute-start(f32[3,32,8,128]{3,2,1,0:T(8,128)} %collective-permute-done.31.refs_30_), channel_id=1, source_target_pairs={{0,1},{1,0},{2,3},{3,2},{4,5},{5,4},{6,7},{7,6},{8,9},{9,8},{10,11... | collective-permute-start | bytes 1179656 | tf_op jit(solution)/shard_map/ppermute | solution.py:13
  124.6 2.8 %collective-permute-start.30 = (f32[3,32,8,128]{3,2,1,0:T(8,128)}, f32[3,32,8,128]{3,2,1,0:T(8,128)}, u32[]{:S(2)}, u32[]{:S(2)}) collective-permute-start(f32[3,32,8,128]{3,2,1,0:T(8,128)} %collective-permute-done.29.refs_28_), channel_id=1, source_target_pairs={{0,1},{1,0},{2,3},{3,2},{4,5},{5,4},{6,7},{7,6},{8,9},{9,8},{10,11... | collective-permute-start | bytes 1179656 | tf_op jit(solution)/shard_map/ppermute | solution.py:13
  (5 other events, 39.7 us)

commit v2 on v0

v2 whole, which is shorter than its diff:
```python
import jax
import jax.numpy as jnp
from jax import lax
from jax.experimental import pallas as pl
from jax.experimental.pallas import tpu as pltpu
from jax.sharding import PartitionSpec as P


CORES = 2
ROWS = 32
UNROLL = 4
SLOTS = 4


class Plan:
    def __init__(self, group, groups, place, count, cells):
        self.group, self.groups, self.count = group, groups, count
        self.chips = count // CORES
        self.chip, self.core = place // CORES, place % CORES
        part = cells // groups
        self.chunks = (part * 3 // 8, part // 2)
        self.share = sum(self.chunks)
        self.rest = groups * self.share
        self.cells = cells
        low = self.chip < self.chips // 2
        near = (self.chip ^ 1, jnp.where(low, 2, 1), jnp.where(low, 3, 0))
        self.begins, self.planes = [], []
        self.note(self.chip, 0, cells)
        for source in near:
            self.note(source, self.rest, cells - self.rest)
        for chunk in range(2):
            for source in near:
                for other in (0, 1, 2, 3):
                    begin = (group ^ other) * self.share + chunk * self.chunks[0]
                    self.note(source, begin, self.chunks[chunk])

    def note(self, source, offset, planes):
        for core in (self.core, 1 - self.core):
            self.begins.append((source * CORES + core) * self.cells + offset)
            self.planes.append(planes)

    def gather(self, velocity, distances, make):
        pairs_of = lambda links: [
            (a * CORES + c, b * CORES + c) for a, b in links for c in range(CORES)
        ]

        def along(value, links):
            return lax.ppermute(value, "gx", pairs_of(links))

        def across(value, bit):
            return lax.ppermute(value, "sep", [(s, s ^ bit) for s in range(self.groups)])

        pieces = []

        def keep(value):
            other = lax.ppermute(value, "gx", [(d, d ^ 1) for d in range(self.count)])
            pieces.extend((value, other))

        inside = jnp.logical_or(self.chip == 1, self.chip == 2)
        mid = [(1, 2), (2, 1)]
        outward = [(1, 0), (2, 3)]

        def line(mine):
            first = along(mine, [(a, a ^ 1) for a in range(self.chips)])
            inner2 = along(mine, mid)
            outer2 = along(inner2, outward)
            inner3 = along(first, mid)
            outer3 = along(inner3, outward)
            return first, jnp.where(inside, inner2, outer2), jnp.where(inside, inner3, outer3)

        keep(velocity)
        for value in line(velocity[:, self.rest :]):
            keep(value)
        for chunk in range(2):
            begin = self.group * self.share + chunk * self.chunks[0]
            mine = lax.dynamic_slice_in_dim(velocity, begin, self.chunks[chunk], 1)
            mine, velocity = lax.optimization_barrier((mine, velocity))
            for slot, value in enumerate(line(mine)):
                tag = f"{slot + 1}{chunk + 1}"
                by_x = across(value, 1)
                by_y = across(value, 2)
                if tag == "31":
                    by_y, distances = lax.optimization_barrier((by_y, distances))
                    table = make(distances)
                if tag == "32":
                    by_y, table = lax.optimization_barrier((by_y, table))
                flip = (slot + chunk) % 2
                diagonal = across(by_y, 1) if flip else across(by_x, 2)
                keep(value)
                keep(by_x)
                keep(by_y)
                keep(diagonal)
        return pieces, table


def tuned(groups, count):
    return groups == 4 and count == 4 * CORES


def kernel(table, spreads, *refs):
    pieces = refs[:-6]
    slopes_out, transport_out, field, staged, sems, out_sems = refs[-6:]
    members, cells = slopes_out.shape[:2]
    rows = staged.shape[3]
    spare = rows + 2
    total = field.shape[1] - spare - SPREAD
    count = len(pieces)
    steps = cells // rows
    begins = members + 3
    needs = begins + count
    queue = needs + count
    until = queue + count

    def copies(number):
        piece = pieces[number]
        begin = table[begins + number]
        short = min(piece.shape[1], SPREAD)
        return (
            pltpu.make_async_copy(
                piece, field.at[:, pl.ds(begin, piece.shape[1])], sems.at[0, number]
            ),
            pltpu.make_async_copy(
                piece.at[:, :short], field.at[:, pl.ds(total + begin, short)], sems.at[1, number]
            ),
            begin < spare,
        )

    def start(number, when):
        @pl.when(when)
        def _():
            whole, again, wraps = copies(number)
            whole.start()
            pl.when(wraps)(again.start)

    for number in range(count):
        start(number, table[needs + number] == 0)
    for number in range(count):
        need = table[needs + number]
        start(number, jnp.logical_and(need > 0, need < steps))

    runs = []
    for number, piece in enumerate(pieces):
        if not runs or runs[-1][0] != piece.shape[1]:
            runs.append([piece.shape[1], number, number])
        runs[-1][2] = number

    def wait(position, carry):
        number = table[queue + position]
        wraps = table[begins + number] < spare
        for planes, least, most in runs:

            @pl.when(jnp.logical_and(number >= least, number <= most))
            def _():
                target = field.at[:, pl.ds(0, planes)]
                pltpu.make_async_copy(target, target, sems.at[0, number]).wait()

                @pl.when(wraps)
                def _():
                    target = field.at[:, pl.ds(0, min(planes, SPREAD))]
                    pltpu.make_async_copy(target, target, sems.at[1, number]).wait()

        return carry

    def write(step, slot):
        rows_out = pl.ds(step * rows, rows)
        return [
            pltpu.make_async_copy(
                staged.at[slot, which], out.at[:, rows_out], out_sems.at[slot, which]
            )
            for which, out in enumerate((slopes_out, transport_out))
        ]

    def spots_of(step):
        result = []
        for distance in [0] + [table[number] for number in range(members + 2)]:
            at = table[members + 2] + step * rows + distance + total - 1
            at = jnp.where(at >= total, at - total, at)
            result.append(jnp.where(at >= total, at - total, at))
        return result

    def plane(spots, x, both):
        base = [field[c, spots[0] + (x + 1)] for c in range(3)]
        fluxes, carried = [], []
        for number in range(members + 2):
            inner = 0 < number <= members
            if not (both or inner):
                continue
            moved = [field[c, spots[number + 1] + (x + 1)] for c in range(3)]
            change = [m - b for m, b in zip(moved, base)]
            squared = change[0] * change[0] + change[1] * change[1] + change[2] * change[2]
            if both:
                fluxes.append(change[0] * squared)
            if inner:
                carried.append((moved[0] + base[0]) * squared)
        if not both:
            return carried
        return carried, [
            (fluxes[member + 2] - fluxes[member]) * spreads[member] for member in range(members)
        ]

    def advance(step, state):
        first = jnp.maximum(table[until + step], table[until + 1])
        lax.fori_loop(first, table[until + step + 1], wait, 0)
        slot = step % SLOTS

        @pl.when(step >= SLOTS)
        def _():
            for copy in write(step - SLOTS, slot):
                copy.wait()

        spots = spots_of(step)

        def turn(index, state):
            before, now, slopes = state
            for u in range(UNROLL):
                x = index * UNROLL + u
                after, following = plane(spots, x + 1, True)
                for member in range(members):
                    staged[slot, 0, member, x] = slopes[member]
                    staged[slot, 1, member, x] = 0.25 * (after[member] - before[member])
                before, now, slopes = now, after, following
            return before, now, slopes

        state = lax.fori_loop(0, rows // UNROLL, turn, state)
        for copy in write(step, slot):
            copy.start()
        return state

    lax.fori_loop(table[until], table[until + 1], wait, 0)
    spots = spots_of(0)
    state = (plane(spots, -1, False), *plane(spots, 0, True))
    lax.fori_loop(0, steps, advance, state)
    for step in range(max(0, steps - SLOTS), steps):
        for copy in write(step, step % SLOTS):
            copy.wait()


SPREAD = 64


def table_of(begins, planes, near, origin, total, rows, steps):
    begins = jnp.stack([jnp.asarray(begin, jnp.int32) for begin in begins])
    number = jnp.arange(len(planes))
    begin = begins[:, None, None]
    size = jnp.asarray(planes, jnp.int32)[:, None, None]
    zero = jnp.zeros((), jnp.int32)
    least = jnp.stack([zero, near[0], near[1], near[-1]])
    most = jnp.stack([zero, near[0], near[-2], near[-1]])
    low = origin - 1 + jnp.arange(steps)[None, :, None] * rows + least
    length = (rows + 2 + most - least)[None, None, :]
    hit = jnp.logical_or((begin - low) % total < length, (low - begin) % total < size)
    hit = jnp.any(hit, axis=2)
    needs = jnp.min(jnp.where(hit, jnp.arange(steps)[None, :], steps), axis=1)
    key = needs * len(planes) + number
    rank = jnp.sum(key[None, :] < key[:, None], axis=1)
    queue = jnp.sum(jnp.where(rank[None, :] == number[:, None], number[None, :], 0), axis=1)
    until = jnp.sum(needs[None, :] < jnp.arange(steps + 1)[:, None], axis=1)
    parts = [near, origin[None], begins, needs, queue, until]
    return jnp.concatenate([part.astype(jnp.int32) for part in parts])


def body(velocity, distances):
    group, groups = lax.axis_index("sep"), lax.axis_size("sep")
    place, count = lax.axis_index("gx"), lax.axis_size("gx")
    cells = velocity.shape[1]
    total = cells * count
    members = distances.shape[0] // groups
    rows = min(ROWS, cells)
    steps = cells // rows
    origin = place * cells

    def make(distances):
        padded = jnp.concatenate([jnp.zeros((1,), jnp.int32), distances, distances[-1:]])
        near = lax.dynamic_slice_in_dim(padded, group * members, members + 2)
        spreads = 1.0 / (near[2:] - near[:-2]).astype(jnp.float32)
        return table_of(begins, planes, near, origin, total, rows, steps), spreads

    if tuned(groups, count):
        plan = Plan(group, groups, place, count, cells)
        begins, planes = plan.begins, plan.planes
        pieces, (table, spreads) = plan.gather(velocity, distances, make)
    else:
        begins, planes = [0], [total]
        pieces = [lax.all_gather(velocity, "gx", axis=1, tiled=True)]
        table, spreads = make(distances)
    window = velocity.shape[2:]
    shape = (members, cells) + window
    smem = pl.BlockSpec(memory_space=pltpu.SMEM)
    whole = pl.BlockSpec(memory_space=pl.ANY)
    return pl.pallas_call(
        kernel,
        out_shape=(jax.ShapeDtypeStruct(shape, jnp.float32),) * 2,
        in_specs=[smem, smem] + [whole] * len(pieces),
        out_specs=(whole, whole),
        scratch_shapes=[
            pltpu.VMEM((velocity.shape[0], total + rows + 2 + SPREAD) + window, jnp.float32),
            pltpu.VMEM((SLOTS, 2, members, rows) + window, jnp.float32),
            pltpu.SemaphoreType.DMA((2, len(pieces))),
            pltpu.SemaphoreType.DMA((SLOTS, 2)),
        ],
        compiler_params=pltpu.CompilerParams(vmem_limit_bytes=56 << 20),
        name="terms",
    )(table, spreads, *pieces)


def solution(mesh):
    placed = (P(None, "gx", None, None), P())
    return jax.shard_map(
        body,
        mesh=mesh,
        in_specs=placed,
        out_specs=(P("sep", "gx", None, None), P("sep", "gx", None, None)),
        check_vma=False,
    )
```

time: 346 us -> 173 us (0.50)
  waiting for transfers between devices: 219 us -> 94.7 us
  other arithmetic: 70 us -> 7.45 us
  starting transfers between devices: 9.15 us -> 47.1 us
  local copies, waits for them, and re-layouts: 27.4 us -> 7.86 us
  between operations: 19.5 us -> 1.26 us
  Pallas kernels: 0 us -> 13 us
    all_gather x1 -> x0, waiting for transfers between devices: 209 us -> none  [body(): whole = lax.all_gather(velocity, 'gx', axis=1, tiled=True)]
    ppermute x4 -> x61, waiting for transfers between devices: 9.54 us -> 94.7 us  [the longest x18 59.2 us: across(): lax.ppermute(value, 'sep', [(s, s ^ bit) for s in range(self.groups)])]
    ppermute x4 -> x61, starting transfers between devices: 9.12 us -> 47.1 us  [the longest x15 25 us: along(): return lax.ppermute(value, 'gx', pairs_of(links))]
    reduce_sum x2 -> x3, other arithmetic: 28.5 us -> 0.4 us  [the longest x1 0.17 us: table_of(): rank = jnp.sum(key[None, :] < key[:, None], axis=1)]
    unnamed x21 -> x0, other arithmetic: 21.6 us -> none
    pallas_call x0 -> x1, Pallas kernels: none -> 13 us  [body(): pl.pallas_call(kernel, out_shape=(jax.ShapeDtypeStruct(shape, jnp.float32...]
    div x1, other arithmetic: 9.98 us -> 0.6 us  [make(): spreads = 1.0 / (near[2:] - near[:-2]).astype(jnp.float32)]
    mul x2 -> x0, other arithmetic: 7.93 us -> none  [terms(): carried = 0.5 * (moved[0] + base[0]) * squared]
  transfers between devices with their start and end apart: 5 -> 61, of which waited for: 2 -> 21; matrix products, arithmetic and copies ran while one was open for 14% -> 7% of each run, Pallas kernels for 0% -> 0%
where the time goes in v2:
time: 173 us; the launch traced here: 171 us
  waiting for transfers between devices  94.7 us (55%)
  starting transfers between devices  47.1 us (27%)
  Pallas kernels  13 us (8%)
  local copies, waits for them, and re-layouts  7.86 us (5%)
  other arithmetic  7.45 us (4%)
    ppermute x18, waiting for transfers between devices, across(): lax.ppermute(value, 'sep', [(s, s ^ bit) for s in range(self.groups)])  59.2 us
    ppermute x15, waiting for transfers between devices, along(): return lax.ppermute(value, 'gx', pairs_of(links))  32.3 us
    ppermute x15, starting transfers between devices, along(): return lax.ppermute(value, 'gx', pairs_of(links))  25 us
    ppermute x18, starting transfers between devices, across(): lax.ppermute(value, 'sep', [(s, s ^ bit) for s in range(self.groups)])  17.9 us
    pallas_call x1, Pallas kernels, body(): pl.pallas_call(kernel, out_shape=(jax.ShapeDtypeStruct(shape, jnp.float32...  13 us
    ppermute x28, starting transfers between devices, keep(): other = lax.ppermute(value, 'gx', [(d, d ^ 1) for d in range(self.count)])  4.09 us
  transfers between devices with their start and end apart: 61, of which 21 were waited for; matrix products, arithmetic and copies ran while one was open for 7% of the time, Pallas kernels for 0%

profile of v2, /device:TPU:4, one launch (start us, length us, event | category | flops | bytes accessed | tf_op | source)
XLA Modules:
  0.0 171.4 jit_solution(9948324977965306816)
XLA Ops:
  0.6 1.9 %constant_dynamic-slice_fusion.1 = f32[3,24,8,128]{3,2,1,0:T(8,128)} fusion(f32[3,256,8,128]{3,2,1,0:T(8,128)} %refs_0_.1, s32[]{:T(128)S(6)} %select_n.79), kind=kLoop, calls=%fused_computation.39 | loop fusion | bytes 589828 | tf_op jit(solution)/shard_map/dynamic_slice | solution.py:76
  2.5 1.4 collective-permute-start.24
  4.9 1.4 collective-permute-start.11
  6.4 4.7 %collective-permute-start.9 = (f32[3,32,8,128]{3,2,1,0:T(8,128)S(1)}, f32[3,32,8,128]{3,2,1,0:T(8,128)}, u32[]{:S(2)}, u32[]{:S(2)}) collective-permute-start(f32[3,32,8,128]{3,2,1,0:T(8,128)S(1)} %slice.35), channel_id=1, source_target_pairs={{0,2},{1,3},{2,0},{3,1},{4,6},{5,7},{6,4},{7,5},{8,10},{9,11},{10,... | collective-permute-start | bytes 1179656 | tf_op jit(solution)/shard_map/ppermute | solution.py:48
  12.1 1.4 collective-permute-start.46
  13.6 4.1 %collective-permute-start = (f32[3,32,8,128]{3,2,1,0:T(8,128)S(1)}, f32[3,32,8,128]{3,2,1,0:T(8,128)}, u32[]{:S(2)}, u32[]{:S(2)}) collective-permute-start(f32[3,32,8,128]{3,2,1,0:T(8,128)S(1)} %constant_dynamic-slice_fusion), channel_id=1, source_target_pairs={{0,2},{1,3},{2,0},{3,1},{4,6},{5,7},{6,4},{7,5},{8,10},{9,11},{10,... | collective-permute-start | bytes 1179656 | tf_op jit(solution)/shard_map/ppermute | solution.py:48
  17.7 9.8 %collective-permute-done.4.refs_8_ = f32[3,24,8,128]{3,2,1,0:T(8,128)} collective-permute-done((f32[3,24,8,128]{3,2,1,0:T(8,128)}, f32[3,24,8,128]{3,2,1,0:T(8,128)}, u32[]{:S(2)}, u32[]{:S(2)}) %collective-permute-start.4) | collective-permute-done | bytes 294944 | tf_op jit(solution)/shard_map/ppermute | solution.py:48
  27.4 1.3 collective-permute-start.25
  29.3 1.5 collective-permute-start.18
  30.8 5.1 %collective-permute-done.refs_32_ = f32[3,32,8,128]{3,2,1,0:T(8,128)} collective-permute-done((f32[3,32,8,128]{3,2,1,0:T(8,128)S(1)}, f32[3,32,8,128]{3,2,1,0:T(8,128)}, u32[]{:S(2)}, u32[]{:S(2)}) %collective-permute-start) | collective-permute-done | bytes 393248 | tf_op jit(solution)/shard_map/ppermute | solution.py:48
  35.8 1.4 collective-permute-start.5
  37.2 3.5 %collective-permute-done.25 = f32[3,24,8,128]{3,2,1,0:T(8,128)} collective-permute-done((f32[3,24,8,128]{3,2,1,0:T(8,128)}, f32[3,24,8,128]{3,2,1,0:T(8,128)}, u32[]{:S(2)}, u32[]{:S(2)}) %collective-permute-start.25) | collective-permute-done | bytes 294944 | tf_op jit(solution)/shard_map/ppermute | solution.py:48
  40.8 1.3 collective-permute-start.12
  42.1 1.4 collective-permute-start.14
  43.5 1.3 collective-permute-start.47
  45.4 8.0 %collective-permute-done.12 = f32[3,32,8,128]{3,2,1,0:T(8,128)} collective-permute-done((f32[3,32,8,128]{3,2,1,0:T(8,128)}, f32[3,32,8,128]{3,2,1,0:T(8,128)}, u32[]{:S(2)}, u32[]{:S(2)}) %collective-permute-start.12) | collective-permute-done | bytes 393248 | tf_op jit(solution)/shard_map/ppermute | solution.py:48
  53.4 1.5 collective-permute-start.40
  55.6 1.4 collective-permute-start.1
  58.0 3.1 %collective-permute-done.47 = f32[3,32,8,128]{3,2,1,0:T(8,128)} collective-permute-done((f32[3,32,8,128]{3,2,1,0:T(8,128)}, f32[3,32,8,128]{3,2,1,0:T(8,128)}, u32[]{:S(2)}, u32[]{:S(2)}) %collective-permute-start.47) | collective-permute-done | bytes 393248 | tf_op jit(solution)/shard_map/ppermute | solution.py:48
  61.6 1.5 collective-permute-start.27
  63.1 1.3 collective-permute-start.6
  64.4 1.6 collective-permute-start.22
  66.0 5.1 %collective-permute-done.29.refs_20_ = f32[3,24,8,128]{3,2,1,0:T(8,128)} collective-permute-done((f32[3,24,8,128]{3,2,1,0:T(8,128)S(1)}, f32[3,24,8,128]{3,2,1,0:T(8,128)}, u32[]{:S(2)}, u32[]{:S(2)}) %collective-permute-start.29) | collective-permute-done | bytes 294944 | tf_op jit(solution)/shard_map/ppermute | solution.py:51
  71.8 1.6 collective-permute-start.31
  73.3 1.4 collective-permute-done.6
  75.8 1.3 collective-permute-start.15
  77.1 1.6 collective-permute-start.7
  78.9 1.0 broadcast_select_fusion.2.refs_4_
  79.9 1.1 collective-permute-done.31.refs_22_
  82.8 3.7 %collective-permute-done.7.refs_28_ = f32[3,24,8,128]{3,2,1,0:T(8,128)S(1)} collective-permute-done((f32[3,24,8,128]{3,2,1,0:T(8,128)S(1)}, f32[3,24,8,128]{3,2,1,0:T(8,128)S(1)}, u32[]{:S(2)}, u32[]{:S(2)}) %collective-permute-start.7) | collective-permute-done | bytes 294944 | tf_op jit(solution)/shard_map/ppermute | solution.py:51
  86.6 1.3 collective-permute-start.2
  87.8 1.5 collective-permute-done.15
  91.5 6.5 %collective-permute-done.34.refs_26_ = f32[3,24,8,128]{3,2,1,0:T(8,128)S(1)} collective-permute-done((f32[3,24,8,128]{3,2,1,0:T(8,128)S(1)}, f32[3,24,8,128]{3,2,1,0:T(8,128)S(1)}, u32[]{:S(2)}, u32[]{:S(2)}) %collective-permute-start.34) | collective-permute-done | bytes 294944 | tf_op jit(solution)/shard_map/ppermute | solution.py:51
  98.0 1.5 collective-permute-start.51
  100.4 1.4 collective-permute-start.44
  102.4 5.4 %collective-permute-done.51.refs_44_ = f32[3,32,8,128]{3,2,1,0:T(8,128)} collective-permute-done((f32[3,32,8,128]{3,2,1,0:T(8,128)S(1)}, f32[3,32,8,128]{3,2,1,0:T(8,128)}, u32[]{:S(2)}, u32[]{:S(2)}) %collective-permute-start.51) | collective-permute-done | bytes 393248 | tf_op jit(solution)/shard_map/ppermute | solution.py:51
  107.9 1.3 add_subtract_fusion
  109.2 2.4 %collective-permute-done.49.refs_42_ = f32[3,32,8,128]{3,2,1,0:T(8,128)} collective-permute-done((f32[3,32,8,128]{3,2,1,0:T(8,128)S(1)}, f32[3,32,8,128]{3,2,1,0:T(8,128)}, u32[]{:S(2)}, u32[]{:S(2)}) %collective-permute-start.49) | collective-permute-done | bytes 393248 | tf_op jit(solution)/shard_map/ppermute | solution.py:51
  112.2 5.5 %collective-permute-done.44.refs_38_ = f32[3,32,8,128]{3,2,1,0:T(8,128)} collective-permute-done((f32[3,32,8,128]{3,2,1,0:T(8,128)}, f32[3,32,8,128]{3,2,1,0:T(8,128)}, u32[]{:S(2)}, u32[]{:S(2)}) %collective-permute-start.44) | collective-permute-done | bytes 393248 | tf_op jit(solution)/shard_map/ppermute | solution.py:51
  119.0 1.5 collective-permute-start.3
  120.5 6.5 %collective-permute-done.37.refs_30_ = f32[3,24,8,128]{3,2,1,0:T(8,128)S(1)} collective-permute-done((f32[3,24,8,128]{3,2,1,0:T(8,128)S(1)}, f32[3,24,8,128]{3,2,1,0:T(8,128)S(1)}, u32[]{:S(2)}, u32[]{:S(2)}) %collective-permute-start.37) | collective-permute-done | bytes 294944 | tf_op jit(solution)/shard_map/ppermute | solution.py:51
  127.2 1.4 collective-permute-done.35.refs_27_
  129.4 4.8 %collective-permute-done.3.refs_52_ = f32[3,32,8,128]{3,2,1,0:T(8,128)} collective-permute-done((f32[3,32,8,128]{3,2,1,0:T(8,128)S(1)}, f32[3,32,8,128]{3,2,1,0:T(8,128)}, u32[]{:S(2)}, u32[]{:S(2)}) %collective-permute-start.3) | collective-permute-done | bytes 393248 | tf_op jit(solution)/shard_map/ppermute | solution.py:51
  136.2 5.1 %collective-permute-done.53.refs_46_ = f32[3,32,8,128]{3,2,1,0:T(8,128)} collective-permute-done((f32[3,32,8,128]{3,2,1,0:T(8,128)}, f32[3,32,8,128]{3,2,1,0:T(8,128)}, u32[]{:S(2)}, u32[]{:S(2)}) %collective-permute-start.53) | collective-permute-done | bytes 393248 | tf_op jit(solution)/shard_map/ppermute | solution.py:51
  142.1 5.8 %collective-permute-done.56.refs_50_ = f32[3,32,8,128]{3,2,1,0:T(8,128)S(1)} collective-permute-done((f32[3,32,8,128]{3,2,1,0:T(8,128)}, f32[3,32,8,128]{3,2,1,0:T(8,128)S(1)}, u32[]{:S(2)}, u32[]{:S(2)}) %collective-permute-start.56) | collective-permute-done | bytes 393248 | tf_op jit(solution)/shard_map/ppermute | solution.py:51
  148.5 7.4 %collective-permute-done.59.refs_54_ = f32[3,32,8,128]{3,2,1,0:T(8,128)S(1)} collective-permute-done((f32[3,32,8,128]{3,2,1,0:T(8,128)}, f32[3,32,8,128]{3,2,1,0:T(8,128)S(1)}, u32[]{:S(2)}, u32[]{:S(2)}) %collective-permute-start.59) | collective-permute-done | bytes 393248 | tf_op jit(solution)/shard_map/ppermute | solution.py:51
  155.9 1.7 collective-permute-done.60.refs_55_
  158.3 13.0 %terms.1 = (f32[8,256,8,128]{3,2,1,0:T(8,128)}, f32[8,256,8,128]{3,2,1,0:T(8,128)}) custom-call(s32[188]{0:T(256)} %concatenate.16.table, f32[8]{0:T(128)} %convert_divide_fusion.spreads, f32[3,256,8,128]{3,2,1,0:T(8,128)} %refs_0_.1, f32[3,256,8,128]{3,2,1,0:T(8,128)} %collective-permute-done.8.refs_1_, f32[3,32,8,128]{3,2,1,0:T(8,128)} %collective-permute-done.9.refs_2_, ...), custom_call_target="tpu_custom_call" | custom-call | tf_op jit(solution)/shard_map/terms/pallas_call | solution.py:290
  (169 shorter events, 19.7 us)
Async XLA Ops:
  2.5 11.1 %collective-permute-start.24 = (f32[3,24,8,128]{3,2,1,0:T(8,128)}, f32[3,24,8,128]{3,2,1,0:T(8,128)}, u32[]{:S(2)}, u32[]{:S(2)}) collective-permute-start(f32[3,24,8,128]{3,2,1,0:T(8,128)} %constant_dynamic-slice_fusion.1), channel_id=1, source_target_pairs={{2,4},{3,5},{4,2},{5,3},{10,12},{11,13},{12,10},{13,11},{18,20},{1... | collective-permute-start | bytes 884744 | tf_op jit(solution)/shard_map/ppermute | solution.py:48
  4.9 23.8 %collective-permute-start.11 = (f32[3,32,8,128]{3,2,1,0:T(8,128)S(1)}, f32[3,32,8,128]{3,2,1,0:T(8,128)}, u32[]{:S(2)}, u32[]{:S(2)}) collective-permute-start(f32[3,32,8,128]{3,2,1,0:T(8,128)S(1)} %slice.35), channel_id=1, source_target_pairs={{2,4},{3,5},{4,2},{5,3},{10,12},{11,13},{12,10},{13,11},{18,20},{1... | collective-permute-start | bytes 1179656 | tf_op jit(solution)/shard_map/ppermute | solution.py:48
  6.4 22.9 %collective-permute-start.9 = (f32[3,32,8,128]{3,2,1,0:T(8,128)S(1)}, f32[3,32,8,128]{3,2,1,0:T(8,128)}, u32[]{:S(2)}, u32[]{:S(2)}) collective-permute-start(f32[3,32,8,128]{3,2,1,0:T(8,128)S(1)} %slice.35), channel_id=1, source_target_pairs={{0,2},{1,3},{2,0},{3,1},{4,6},{5,7},{6,4},{7,5},{8,10},{9,11},{10,... | collective-permute-start | bytes 1179656 | tf_op jit(solution)/shard_map/ppermute | solution.py:48
  11.0 16.4 %collective-permute-start.4 = (f32[3,24,8,128]{3,2,1,0:T(8,128)}, f32[3,24,8,128]{3,2,1,0:T(8,128)}, u32[]{:S(2)}, u32[]{:S(2)}) collective-permute-start(f32[3,24,8,128]{3,2,1,0:T(8,128)} %constant_dynamic-slice_fusion.1), channel_id=1, source_target_pairs={{0,2},{1,3},{2,0},{3,1},{4,6},{5,7},{6,4},{7,5},{8,10},{9,11},{10,... | collective-permute-start | bytes 884744 | tf_op jit(solution)/shard_map/ppermute | solution.py:48
  12.1 18.6 %collective-permute-start.46 = (f32[3,32,8,128]{3,2,1,0:T(8,128)S(1)}, f32[3,32,8,128]{3,2,1,0:T(8,128)}, u32[]{:S(2)}, u32[]{:S(2)}) collective-permute-start(f32[3,32,8,128]{3,2,1,0:T(8,128)S(1)} %constant_dynamic-slice_fusion), channel_id=1, source_target_pairs={{2,4},{3,5},{4,2},{5,3},{10,12},{11,13},{12,10},{13,11},{18,20},{1... | collective-permute-start | bytes 1179656 | tf_op jit(solution)/shard_map/ppermute | solution.py:48
  13.6 22.3 %collective-permute-start = (f32[3,32,8,128]{3,2,1,0:T(8,128)S(1)}, f32[3,32,8,128]{3,2,1,0:T(8,128)}, u32[]{:S(2)}, u32[]{:S(2)}) collective-permute-start(f32[3,32,8,128]{3,2,1,0:T(8,128)S(1)} %constant_dynamic-slice_fusion), channel_id=1, source_target_pairs={{0,2},{1,3},{2,0},{3,1},{4,6},{5,7},{6,4},{7,5},{8,10},{9,11},{10,... | collective-permute-start | bytes 1179656 | tf_op jit(solution)/shard_map/ppermute | solution.py:48
  27.4 13.3 %collective-permute-start.25 = (f32[3,24,8,128]{3,2,1,0:T(8,128)}, f32[3,24,8,128]{3,2,1,0:T(8,128)}, u32[]{:S(2)}, u32[]{:S(2)}) collective-permute-start(f32[3,24,8,128]{3,2,1,0:T(8,128)} %collective-permute-done.24), channel_id=1, source_target_pairs={{2,0},{3,1},{4,6},{5,7},{10,8},{11,9},{12,14},{13,15},{18,16},{19,... | collective-permute-start | bytes 884744 | tf_op jit(solution)/shard_map/ppermute | solution.py:48
  28.7 13.3 %collective-permute-start.20 = (f32[3,24,8,128]{3,2,1,0:T(8,128)}, f32[3,24,8,128]{3,2,1,0:T(8,128)}, u32[]{:S(2)}, u32[]{:S(2)}) collective-permute-start(f32[3,24,8,128]{3,2,1,0:T(8,128)} %collective-permute-done.4.refs_8_), channel_id=1, source_target_pairs={{0,16},{8,24},{16,0},{24,8},{1,17},{9,25},{17,1},{25,9},{2,18},{10... | collective-permute-start | bytes 884744 | tf_op jit(solution)/shard_map/ppermute | solution.py:51
  29.3 14.2 %collective-permute-start.18 = (f32[3,24,8,128]{3,2,1,0:T(8,128)}, f32[3,24,8,128]{3,2,1,0:T(8,128)}, u32[]{:S(2)}, u32[]{:S(2)}) collective-permute-start(f32[3,24,8,128]{3,2,1,0:T(8,128)} %collective-permute-done.4.refs_8_), channel_id=1, source_target_pairs={{0,8},{8,0},{16,24},{24,16},{1,9},{9,1},{17,25},{25,17},{2,10},{10... | collective-permute-start | bytes 884744 | tf_op jit(solution)/shard_map/ppermute | solution.py:51
  30.8 12.7 %collective-permute-start.17 = (f32[3,24,8,128]{3,2,1,0:T(8,128)}, f32[3,24,8,128]{3,2,1,0:T(8,128)}, u32[]{:S(2)}, u32[]{:S(2)}) collective-permute-start(f32[3,24,8,128]{3,2,1,0:T(8,128)} %collective-permute-done.4.refs_8_), channel_id=1, source_target_pairs={{0,1},{1,0},{2,3},{3,2},{4,5},{5,4},{6,7},{7,6},{8,9},{9,8},{10,11... | collective-permute-start | bytes 884744 | tf_op jit(solution)/shard_map/ppermute | solution.py:56
  35.8 8.9 %collective-permute-start.5 = (f32[3,24,8,128]{3,2,1,0:T(8,128)}, f32[3,24,8,128]{3,2,1,0:T(8,128)}, u32[]{:S(2)}, u32[]{:S(2)}) collective-permute-start(f32[3,24,8,128]{3,2,1,0:T(8,128)} %collective-permute-done.4.refs_8_), channel_id=1, source_target_pairs={{2,4},{3,5},{4,2},{5,3},{10,12},{11,13},{12,10},{13,11},{18,20},{1... | collective-permute-start | bytes 884744 | tf_op jit(solution)/shard_map/ppermute | solution.py:48
  40.8 12.6 %collective-permute-start.12 = (f32[3,32,8,128]{3,2,1,0:T(8,128)}, f32[3,32,8,128]{3,2,1,0:T(8,128)}, u32[]{:S(2)}, u32[]{:S(2)}) collective-permute-start(f32[3,32,8,128]{3,2,1,0:T(8,128)} %collective-permute-done.11), channel_id=1, source_target_pairs={{2,0},{3,1},{4,6},{5,7},{10,8},{11,9},{12,14},{13,15},{18,16},{19,... | collective-permute-start | bytes 1179656 | tf_op jit(solution)/shard_map/ppermute | solution.py:48
  42.1 12.8 %collective-permute-start.14 = (f32[3,32,8,128]{3,2,1,0:T(8,128)}, f32[3,32,8,128]{3,2,1,0:T(8,128)}, u32[]{:S(2)}, u32[]{:S(2)}) collective-permute-start(f32[3,32,8,128]{3,2,1,0:T(8,128)} %collective-permute-done.9.refs_2_), channel_id=1, source_target_pairs={{2,4},{3,5},{4,2},{5,3},{10,12},{11,13},{12,10},{13,11},{18,20},{1... | collective-permute-start | bytes 1179656 | tf_op jit(solution)/shard_map/ppermute | solution.py:48
  43.5 11.4 %collective-permute-start.10 = (f32[3,32,8,128]{3,2,1,0:T(8,128)}, f32[3,32,8,128]{3,2,1,0:T(8,128)S(1)}, u32[]{:S(2)}, u32[]{:S(2)}) collective-permute-start(f32[3,32,8,128]{3,2,1,0:T(8,128)} %collective-permute-done.9.refs_2_), channel_id=1, source_target_pairs={{0,1},{1,0},{2,3},{3,2},{4,5},{5,4},{6,7},{7,6},{8,9},{9,8},{10,11... | collective-permute-start | bytes 1179656 | tf_op jit(solution)/shard_map/ppermute | solution.py:56
  43.5 17.6 %collective-permute-start.47 = (f32[3,32,8,128]{3,2,1,0:T(8,128)}, f32[3,32,8,128]{3,2,1,0:T(8,128)}, u32[]{:S(2)}, u32[]{:S(2)}) collective-permute-start(f32[3,32,8,128]{3,2,1,0:T(8,128)} %collective-permute-done.46), channel_id=1, source_target_pairs={{2,0},{3,1},{4,6},{5,7},{10,8},{11,9},{12,14},{13,15},{18,16},{19,... | collective-permute-start | bytes 1179656 | tf_op jit(solution)/shard_map/ppermute | solution.py:48
  44.8 16.8 %collective-permute-start.42 = (f32[3,32,8,128]{3,2,1,0:T(8,128)}, f32[3,32,8,128]{3,2,1,0:T(8,128)}, u32[]{:S(2)}, u32[]{:S(2)}) collective-permute-start(f32[3,32,8,128]{3,2,1,0:T(8,128)} %collective-permute-done.refs_32_), channel_id=1, source_target_pairs={{0,16},{8,24},{16,0},{24,8},{1,17},{9,25},{17,1},{25,9},{2,18},{10... | collective-permute-start | bytes 1179656 | tf_op jit(solution)/shard_map/ppermute | solution.py:51
  53.4 9.7 %collective-permute-start.40 = (f32[3,32,8,128]{3,2,1,0:T(8,128)}, f32[3,32,8,128]{3,2,1,0:T(8,128)}, u32[]{:S(2)}, u32[]{:S(2)}) collective-permute-start(f32[3,32,8,128]{3,2,1,0:T(8,128)} %collective-permute-done.refs_32_), channel_id=1, source_target_pairs={{0,8},{8,0},{16,24},{24,16},{1,9},{9,1},{17,25},{25,17},{2,10},{10... | collective-permute-start | bytes 1179656 | tf_op jit(solution)/shard_map/ppermute | solution.py:51
  54.9 8.3 %collective-permute-start.39 = (f32[3,32,8,128]{3,2,1,0:T(8,128)}, f32[3,32,8,128]{3,2,1,0:T(8,128)}, u32[]{:S(2)}, u32[]{:S(2)}) collective-permute-start(f32[3,32,8,128]{3,2,1,0:T(8,128)} %collective-permute-done.refs_32_), channel_id=1, source_target_pairs={{0,1},{1,0},{2,3},{3,2},{4,5},{5,4},{6,7},{7,6},{8,9},{9,8},{10,11... | collective-permute-start | bytes 1179656 | tf_op jit(solution)/shard_map/ppermute | solution.py:56
  55.6 8.8 %collective-permute-start.1 = (f32[3,32,8,128]{3,2,1,0:T(8,128)}, f32[3,32,8,128]{3,2,1,0:T(8,128)}, u32[]{:S(2)}, u32[]{:S(2)}) collective-permute-start(f32[3,32,8,128]{3,2,1,0:T(8,128)} %collective-permute-done.refs_32_), channel_id=1, source_target_pairs={{2,4},{3,5},{4,2},{5,3},{10,12},{11,13},{12,10},{13,11},{18,20},{1... | collective-permute-start | bytes 1179656 | tf_op jit(solution)/shard_map/ppermute | solution.py:48
  61.1 10.0 %collective-permute-start.29 = (f32[3,24,8,128]{3,2,1,0:T(8,128)S(1)}, f32[3,24,8,128]{3,2,1,0:T(8,128)}, u32[]{:S(2)}, u32[]{:S(2)}) collective-permute-start(f32[3,24,8,128]{3,2,1,0:T(8,128)S(1)} %broadcast_select_fusion.4.refs_16_), channel_id=1, source_target_pairs={{0,16},{8,24},{16,0},{24,8},{1,17},{9,25},{17,1},{25,9},{2,18},{10... | collective-permute-start | bytes 884744 | tf_op jit(solution)/shard_map/ppermute | solution.py:51
  61.6 9.5 %collective-permute-start.27 = (f32[3,24,8,128]{3,2,1,0:T(8,128)S(1)}, f32[3,24,8,128]{3,2,1,0:T(8,128)}, u32[]{:S(2)}, u32[]{:S(2)}) collective-permute-start(f32[3,24,8,128]{3,2,1,0:T(8,128)S(1)} %broadcast_select_fusion.4.refs_16_), channel_id=1, source_target_pairs={{0,8},{8,0},{16,24},{24,16},{1,9},{9,1},{17,25},{25,17},{2,10},{10... | collective-permute-start | bytes 884744 | tf_op jit(solution)/shard_map/ppermute | solution.py:51
  63.1 8.6 %collective-permute-start.26 = (f32[3,24,8,128]{3,2,1,0:T(8,128)S(1)}, f32[3,24,8,128]{3,2,1,0:T(8,128)}, u32[]{:S(2)}, u32[]{:S(2)}) collective-permute-start(f32[3,24,8,128]{3,2,1,0:T(8,128)S(1)} %broadcast_select_fusion.4.refs_16_), channel_id=1, source_target_pairs={{0,1},{1,0},{2,3},{3,2},{4,5},{5,4},{6,7},{7,6},{8,9},{9,8},{10,11... | collective-permute-start | bytes 884744 | tf_op jit(solution)/shard_map/ppermute | solution.py:56
  63.1 11.6 %collective-permute-start.6 = (f32[3,24,8,128]{3,2,1,0:T(8,128)}, f32[3,24,8,128]{3,2,1,0:T(8,128)}, u32[]{:S(2)}, u32[]{:S(2)}) collective-permute-start(f32[3,24,8,128]{3,2,1,0:T(8,128)} %collective-permute-done.5), channel_id=1, source_target_pairs={{2,0},{3,1},{4,6},{5,7},{10,8},{11,9},{12,14},{13,15},{18,16},{19,... | collective-permute-start | bytes 884744 | tf_op jit(solution)/shard_map/ppermute | solution.py:48
  64.4 12.6 %collective-permute-start.22 = (f32[3,24,8,128]{3,2,1,0:T(8,128)}, f32[3,24,8,128]{3,2,1,0:T(8,128)}, u32[]{:S(2)}, u32[]{:S(2)}) collective-permute-start(f32[3,24,8,128]{3,2,1,0:T(8,128)} %collective-permute-done.18.refs_10_), channel_id=1, source_target_pairs={{0,16},{8,24},{16,0},{24,8},{1,17},{9,25},{17,1},{25,9},{2,18},{10... | collective-permute-start | bytes 884744 | tf_op jit(solution)/shard_map/ppermute | solution.py:51
  71.8 9.3 %collective-permute-start.31 = (f32[3,24,8,128]{3,2,1,0:T(8,128)}, f32[3,24,8,128]{3,2,1,0:T(8,128)S(1)}, u32[]{:S(2)}, u32[]{:S(2)}) collective-permute-start(f32[3,24,8,128]{3,2,1,0:T(8,128)} %collective-permute-done.29.refs_20_), channel_id=1, source_target_pairs={{0,8},{8,0},{16,24},{24,16},{1,9},{9,1},{17,25},{25,17},{2,10},{10... | collective-permute-start | bytes 884744 | tf_op jit(solution)/shard_map/ppermute | solution.py:51
  75.8 13.6 %collective-permute-start.15 = (f32[3,32,8,128]{3,2,1,0:T(8,128)}, f32[3,32,8,128]{3,2,1,0:T(8,128)S(1)}, u32[]{:S(2)}, u32[]{:S(2)}) collective-permute-start(f32[3,32,8,128]{3,2,1,0:T(8,128)} %collective-permute-done.14), channel_id=1, source_target_pairs={{2,0},{3,1},{4,6},{5,7},{10,8},{11,9},{12,14},{13,15},{18,16},{19,... | collective-permute-start | bytes 1179656 | tf_op jit(solution)/shard_map/ppermute | solution.py:48
  77.1 9.5 %collective-permute-start.7 = (f32[3,24,8,128]{3,2,1,0:T(8,128)S(1)}, f32[3,24,8,128]{3,2,1,0:T(8,128)S(1)}, u32[]{:S(2)}, u32[]{:S(2)}) collective-permute-start(f32[3,24,8,128]{3,2,1,0:T(8,128)S(1)} %broadcast_select_fusion.5.refs_24_), channel_id=1, source_target_pairs={{0,16},{8,24},{16,0},{24,8},{1,17},{9,25},{17,1},{25,9},{2,18},{10... | collective-permute-start | bytes 884744 | tf_op jit(solution)/shard_map/ppermute | solution.py:51
  81.1 76.5 %collective-permute-start.8 = (f32[3,256,8,128]{3,2,1,0:T(8,128)S(1)}, f32[3,256,8,128]{3,2,1,0:T(8,128)}, u32[]{:S(2)}, u32[]{:S(2)}) collective-permute-start(f32[3,256,8,128]{3,2,1,0:T(8,128)S(1)} %copy-done), channel_id=1, source_target_pairs={{0,1},{1,0},{2,3},{3,2},{4,5},{5,4},{6,7},{7,6},{8,9},{9,8},{10,11... | collective-permute-start | bytes 9437192 | tf_op jit(solution)/shard_map/ppermute | solution.py:56
  81.1 9.6 %collective-permute-start.23 = (f32[3,24,8,128]{3,2,1,0:T(8,128)}, f32[3,24,8,128]{3,2,1,0:T(8,128)S(1)}, u32[]{:S(2)}, u32[]{:S(2)}) collective-permute-start(f32[3,24,8,128]{3,2,1,0:T(8,128)} %collective-permute-done.22.refs_14_), channel_id=1, source_target_pairs={{0,1},{1,0},{2,3},{3,2},{4,5},{5,4},{6,7},{7,6},{8,9},{9,8},{10,11... | collective-permute-start | bytes 884744 | tf_op jit(solution)/shard_map/ppermute | solution.py:56
  82.7 17.6 %collective-permute-start.13 = (f32[3,32,8,128]{3,2,1,0:T(8,128)S(1)}, f32[3,32,8,128]{3,2,1,0:T(8,128)S(1)}, u32[]{:S(2)}, u32[]{:S(2)}) collective-permute-start(f32[3,32,8,128]{3,2,1,0:T(8,128)S(1)} %broadcast_select_fusion.2.refs_4_), channel_id=1, source_target_pairs={{0,1},{1,0},{2,3},{3,2},{4,5},{5,4},{6,7},{7,6},{8,9},{9,8},{10,11... | collective-permute-start | bytes 1179656 | tf_op jit(solution)/shard_map/ppermute | solution.py:56
  86.6 13.8 %collective-permute-start.2 = (f32[3,32,8,128]{3,2,1,0:T(8,128)}, f32[3,32,8,128]{3,2,1,0:T(8,128)S(1)}, u32[]{:S(2)}, u32[]{:S(2)}) collective-permute-start(f32[3,32,8,128]{3,2,1,0:T(8,128)} %collective-permute-done.1), channel_id=1, source_target_pairs={{2,0},{3,1},{4,6},{5,7},{10,8},{11,9},{12,14},{13,15},{18,16},{19,... | collective-permute-start | bytes 1179656 | tf_op jit(solution)/shard_map/ppermute | solution.py:48
  89.4 8.6 %collective-permute-start.34 = (f32[3,24,8,128]{3,2,1,0:T(8,128)S(1)}, f32[3,24,8,128]{3,2,1,0:T(8,128)S(1)}, u32[]{:S(2)}, u32[]{:S(2)}) collective-permute-start(f32[3,24,8,128]{3,2,1,0:T(8,128)S(1)} %broadcast_select_fusion.5.refs_24_), channel_id=1, source_target_pairs={{0,8},{8,0},{16,24},{24,16},{1,9},{9,1},{17,25},{25,17},{2,10},{10... | collective-permute-start | bytes 884744 | tf_op jit(solution)/shard_map/ppermute | solution.py:51
  90.6 8.9 %collective-permute-start.33 = (f32[3,24,8,128]{3,2,1,0:T(8,128)S(1)}, f32[3,24,8,128]{3,2,1,0:T(8,128)S(1)}, u32[]{:S(2)}, u32[]{:S(2)}) collective-permute-start(f32[3,24,8,128]{3,2,1,0:T(8,128)S(1)} %broadcast_select_fusion.5.refs_24_), channel_id=1, source_target_pairs={{0,1},{1,0},{2,3},{3,2},{4,5},{5,4},{6,7},{7,6},{8,9},{9,8},{10,11... | collective-permute-start | bytes 884744 | tf_op jit(solution)/shard_map/ppermute | solution.py:56
  98.0 9.9 %collective-permute-start.51 = (f32[3,32,8,128]{3,2,1,0:T(8,128)S(1)}, f32[3,32,8,128]{3,2,1,0:T(8,128)}, u32[]{:S(2)}, u32[]{:S(2)}) collective-permute-start(f32[3,32,8,128]{3,2,1,0:T(8,128)S(1)} %broadcast_select_fusion.refs_40_), channel_id=1, source_target_pairs={{0,16},{8,24},{16,0},{24,8},{1,17},{9,25},{17,1},{25,9},{2,18},{10... | collective-permute-start | bytes 1179656 | tf_op jit(solution)/shard_map/ppermute | solution.py:51
  99.6 12.1 %collective-permute-start.49 = (f32[3,32,8,128]{3,2,1,0:T(8,128)S(1)}, f32[3,32,8,128]{3,2,1,0:T(8,128)}, u32[]{:S(2)}, u32[]{:S(2)}) collective-permute-start(f32[3,32,8,128]{3,2,1,0:T(8,128)S(1)} %broadcast_select_fusion.refs_40_), channel_id=1, source_target_pairs={{0,8},{8,0},{16,24},{24,16},{1,9},{9,1},{17,25},{25,17},{2,10},{10... | collective-permute-start | bytes 1179656 | tf_op jit(solution)/shard_map/ppermute | solution.py:51
  100.3 11.4 %collective-permute-start.48 = (f32[3,32,8,128]{3,2,1,0:T(8,128)S(1)}, f32[3,32,8,128]{3,2,1,0:T(8,128)S(1)}, u32[]{:S(2)}, u32[]{:S(2)}) collective-permute-start(f32[3,32,8,128]{3,2,1,0:T(8,128)S(1)} %broadcast_select_fusion.refs_40_), channel_id=1, source_target_pairs={{0,1},{1,0},{2,3},{3,2},{4,5},{5,4},{6,7},{7,6},{8,9},{9,8},{10,11... | collective-permute-start | bytes 1179656 | tf_op jit(solution)/shard_map/ppermute | solution.py:56
  100.4 17.3 %collective-permute-start.44 = (f32[3,32,8,128]{3,2,1,0:T(8,128)}, f32[3,32,8,128]{3,2,1,0:T(8,128)}, u32[]{:S(2)}, u32[]{:S(2)}) collective-permute-start(f32[3,32,8,128]{3,2,1,0:T(8,128)} %collective-permute-done.42.refs_36_), channel_id=1, source_target_pairs={{0,8},{8,0},{16,24},{24,16},{1,9},{9,1},{17,25},{25,17},{2,10},{10... | collective-permute-start | bytes 1179656 | tf_op jit(solution)/shard_map/ppermute | solution.py:51
  107.9 10.4 %collective-permute-start.43 = (f32[3,32,8,128]{3,2,1,0:T(8,128)}, f32[3,32,8,128]{3,2,1,0:T(8,128)S(1)}, u32[]{:S(2)}, u32[]{:S(2)}) collective-permute-start(f32[3,32,8,128]{3,2,1,0:T(8,128)} %collective-permute-done.42.refs_36_), channel_id=1, source_target_pairs={{0,1},{1,0},{2,3},{3,2},{4,5},{5,4},{6,7},{7,6},{8,9},{9,8},{10,11... | collective-permute-start | bytes 1179656 | tf_op jit(solution)/shard_map/ppermute | solution.py:56
  117.6 9.4 %collective-permute-start.37 = (f32[3,24,8,128]{3,2,1,0:T(8,128)S(1)}, f32[3,24,8,128]{3,2,1,0:T(8,128)S(1)}, u32[]{:S(2)}, u32[]{:S(2)}) collective-permute-start(f32[3,24,8,128]{3,2,1,0:T(8,128)S(1)} %collective-permute-done.34.refs_26_), channel_id=1, source_target_pairs={{0,16},{8,24},{16,0},{24,8},{1,17},{9,25},{17,1},{25,9},{2,18},{10... | collective-permute-start | bytes 884744 | tf_op jit(solution)/shard_map/ppermute | solution.py:51
  118.3 10.5 %collective-permute-start.16 = (f32[3,32,8,128]{3,2,1,0:T(8,128)S(1)}, f32[3,32,8,128]{3,2,1,0:T(8,128)S(1)}, u32[]{:S(2)}, u32[]{:S(2)}) collective-permute-start(f32[3,32,8,128]{3,2,1,0:T(8,128)S(1)} %broadcast_select_fusion.1.refs_6_), channel_id=1, source_target_pairs={{0,1},{1,0},{2,3},{3,2},{4,5},{5,4},{6,7},{7,6},{8,9},{9,8},{10,11... | collective-permute-start | bytes 1179656 | tf_op jit(solution)/shard_map/ppermute | solution.py:56
  118.4 10.1 %collective-permute-start.36 = (f32[3,24,8,128]{3,2,1,0:T(8,128)S(1)}, f32[3,24,8,128]{3,2,1,0:T(8,128)S(1)}, u32[]{:S(2)}, u32[]{:S(2)}) collective-permute-start(f32[3,24,8,128]{3,2,1,0:T(8,128)S(1)} %collective-permute-done.7.refs_28_), channel_id=1, source_target_pairs={{0,1},{1,0},{2,3},{3,2},{4,5},{5,4},{6,7},{7,6},{8,9},{9,8},{10,11... | collective-permute-start | bytes 884744 | tf_op jit(solution)/shard_map/ppermute | solution.py:56
  119.0 15.1 %collective-permute-start.3 = (f32[3,32,8,128]{3,2,1,0:T(8,128)S(1)}, f32[3,32,8,128]{3,2,1,0:T(8,128)}, u32[]{:S(2)}, u32[]{:S(2)}) collective-permute-start(f32[3,32,8,128]{3,2,1,0:T(8,128)S(1)} %broadcast_select_fusion.3.refs_48_), channel_id=1, source_target_pairs={{0,16},{8,24},{16,0},{24,8},{1,17},{9,25},{17,1},{25,9},{2,18},{10... | collective-permute-start | bytes 1179656 | tf_op jit(solution)/shard_map/ppermute | solution.py:51
  128.6 12.7 %collective-permute-start.53 = (f32[3,32,8,128]{3,2,1,0:T(8,128)}, f32[3,32,8,128]{3,2,1,0:T(8,128)}, u32[]{:S(2)}, u32[]{:S(2)}) collective-permute-start(f32[3,32,8,128]{3,2,1,0:T(8,128)} %collective-permute-done.49.refs_42_), channel_id=1, source_target_pairs={{0,16},{8,24},{16,0},{24,8},{1,17},{9,25},{17,1},{25,9},{2,18},{10... | collective-permute-start | bytes 1179656 | tf_op jit(solution)/shard_map/ppermute | solution.py:51
  128.6 12.7 %collective-permute-start.50 = (f32[3,32,8,128]{3,2,1,0:T(8,128)}, f32[3,32,8,128]{3,2,1,0:T(8,128)}, u32[]{:S(2)}, u32[]{:S(2)}) collective-permute-start(f32[3,32,8,128]{3,2,1,0:T(8,128)} %collective-permute-done.49.refs_42_), channel_id=1, source_target_pairs={{0,1},{1,0},{2,3},{3,2},{4,5},{5,4},{6,7},{7,6},{8,9},{9,8},{10,11... | collective-permute-start | bytes 1179656 | tf_op jit(solution)/shard_map/ppermute | solution.py:56
  135.7 12.2 %collective-permute-start.56 = (f32[3,32,8,128]{3,2,1,0:T(8,128)}, f32[3,32,8,128]{3,2,1,0:T(8,128)S(1)}, u32[]{:S(2)}, u32[]{:S(2)}) collective-permute-start(f32[3,32,8,128]{3,2,1,0:T(8,128)} %copy-done.4), channel_id=1, source_target_pairs={{0,8},{8,0},{16,24},{24,16},{1,9},{9,1},{17,25},{25,17},{2,10},{10... | collective-permute-start | bytes 1179656 | tf_op jit(solution)/shard_map/ppermute | solution.py:51
  141.3 14.5 %collective-permute-start.59 = (f32[3,32,8,128]{3,2,1,0:T(8,128)}, f32[3,32,8,128]{3,2,1,0:T(8,128)S(1)}, u32[]{:S(2)}, u32[]{:S(2)}) collective-permute-start(f32[3,32,8,128]{3,2,1,0:T(8,128)} %collective-permute-done.3.refs_52_), channel_id=1, source_target_pairs={{0,8},{8,0},{16,24},{24,16},{1,9},{9,1},{17,25},{25,17},{2,10},{10... | collective-permute-start | bytes 1179656 | tf_op jit(solution)/shard_map/ppermute | solution.py:51
  147.9 8.0 %collective-permute-start.58 = (f32[3,32,8,128]{3,2,1,0:T(8,128)}, f32[3,32,8,128]{3,2,1,0:T(8,128)S(1)}, u32[]{:S(2)}, u32[]{:S(2)}) collective-permute-start(f32[3,32,8,128]{3,2,1,0:T(8,128)} %collective-permute-done.3.refs_52_), channel_id=1, source_target_pairs={{0,1},{1,0},{2,3},{3,2},{4,5},{5,4},{6,7},{7,6},{8,9},{9,8},{10,11... | collective-permute-start | bytes 1179656 | tf_op jit(solution)/shard_map/ppermute | solution.py:56
  147.9 8.0 %collective-permute-start.54 = (f32[3,32,8,128]{3,2,1,0:T(8,128)}, f32[3,32,8,128]{3,2,1,0:T(8,128)S(1)}, u32[]{:S(2)}, u32[]{:S(2)}) collective-permute-start(f32[3,32,8,128]{3,2,1,0:T(8,128)} %collective-permute-done.53.refs_46_), channel_id=1, source_target_pairs={{0,1},{1,0},{2,3},{3,2},{4,5},{5,4},{6,7},{7,6},{8,9},{9,8},{10,11... | collective-permute-start | bytes 1179656 | tf_op jit(solution)/shard_map/ppermute | solution.py:56
  (47 other events, 846.2 us)
